TPU v7x, 512 devices: a whole 4x4x16 slice. The times are simulated.
512 devices in a mesh: ctx: 64 (over y, z_hi, x, core), head: 8 (over z_lo).
Axes of the slice: x: 4, y: 4, z: 16 (z_hi: 2, z_lo: 8; z = z_hi * 8 + z_lo), core: 2. Of those that a mesh axis runs over, the one named last changes fastest.
Arguments:
- query_raw: bfloat16 [16384, 5120], P('ctx', 'head'), may hold values from -9 to 9
- key_raw: bfloat16 [16384, 5120], P('ctx', 'head'), may hold values from -9 to 9
- values: bfloat16 [16384, 5120], P('ctx', 'head'), may hold values from -6 to 6
- out_grad: bfloat16 [16384, 5120], P('ctx', 'head'), may hold values from -128 to 128
- query_gain: float32 [5120], P('head'), may hold values from 0.25 to 1.75
- key_gain: float32 [5120], P('head'), may hold values from 0.25 to 1.75
- key_tiles: int32 [128, 4], P('ctx'), may hold values from 0 to 127, as said below
- global_ids: int32 [128], P('ctx'), may hold values from 0 to 16383, as said below
- readers: int32 [64, 64], P('ctx'), may hold values from 0 to 1, as said below
Outputs:
- query_grad: bfloat16 [16384, 5120], P('ctx', 'head')
- key_grad: bfloat16 [16384, 5120], P('ctx', 'head')
- value_grad: bfloat16 [16384, 5120], P('ctx', 'head')
Inputs may be any that keep to these rules, and one draw needn't show every extreme that they name: `key_tiles`: row t lists, ascending, the 4 tiles of 4 consecutive tile-frames of 1 tiles; every listed tile lies on an index of ctx at most 1 away from tile t's, and in every draw some tile reads a tile exactly 1 below and some tile one exactly 1 above. `global_ids`: entries c * 2 to (c + 1) * 2 - 1 are distinct ascending tokens of index c of ctx. `readers`: each row has either one 1 or all 64 entries 1; at least one row has all.
All inputs are finite; a program needn't handle non-finite values.
Results may differ from a plain program's by a relative error of at most 0.02.
Values may be sent and summed in bfloat16 or wider, within the bound.
A program may use at most 64 MiB of HBM per device.

v0:
```python
import jax
import jax.numpy as jnp
from jax import lax
from jax.sharding import PartitionSpec as P

HEAD_DIM = 128
D = 5120
TILE = 128
REACH = 1
G_DEV = 2


EPSILON = 1e-06


def passed_along(shard, axis, by):
    count = lax.axis_size(axis)
    return lax.ppermute(shard, axis, [(i, (i + by) % count) for i in range(count)])


def normalize(as_float, gain, squares):
    inverse = lax.rsqrt(squares[:, None] / D + EPSILON)
    return (inverse, (as_float * inverse * gain).astype(jnp.bfloat16))


def norm_grad(as_float, inverse, scaled, coeffs):
    return (inverse * scaled - as_float * inverse**3 * (coeffs[:, None] / D)).astype(jnp.bfloat16)


def body(
    query_raw, key_raw, values, out_grad, query_gain, key_gain, key_tiles, global_ids, readers
):
    tokens_here, width_here = query_raw.shape
    heads_here = width_here // HEAD_DIM
    tiles_here = tokens_here // TILE
    factor = HEAD_DIM ** (-0.5)
    device = lax.axis_index("ctx")
    query_rows = query_raw.astype(jnp.float32)
    key_rows = key_raw.astype(jnp.float32)
    query_sq, key_sq = lax.psum(
        (jnp.sum(query_rows * query_rows, axis=1), jnp.sum(key_rows * key_rows, axis=1)), "head"
    )
    query_inv, query_norm = normalize(query_rows, query_gain, query_sq)
    key_inv, key_norm = normalize(key_rows, key_gain, key_sq)
    own_rows = global_ids - device * tokens_here
    own_pair = jnp.stack([key_norm[own_rows], values[own_rows]])
    global_pair = lax.all_gather(own_pair, "ctx", axis=1, tiled=True)
    global_keys = global_pair[0].reshape(-1, heads_here, HEAD_DIM)
    global_vals = global_pair[1].reshape(-1, heads_here, HEAD_DIM)
    live_mask = jnp.repeat(readers[0] > 0, G_DEV)
    key_value = jnp.stack([key_norm, values])
    current = passed_along(key_value, "ctx", -REACH)
    pieces = [current]
    for hop_index in range(2 * REACH):
        current = passed_along(current, "ctx", 1)
        pieces.append(current)
    pieces = pieces[::-1]
    window_pair = jnp.concatenate(pieces, axis=1)
    first_tile = (device - REACH) * tiles_here
    local_tiles = key_tiles - first_tile
    window_rows = (
        local_tiles[:, :, None] * TILE + jnp.arange(TILE, dtype=jnp.int32)[None, None, :]
    ).reshape(tiles_here, -1)
    window_count = window_rows.shape[1]
    window_keys = window_pair[0][window_rows].reshape(
        tiles_here, window_count, heads_here, HEAD_DIM
    )
    window_vals = window_pair[1][window_rows].reshape(
        tiles_here, window_count, heads_here, HEAD_DIM
    )
    query_four = query_norm.reshape(tiles_here, TILE, heads_here, HEAD_DIM)
    grad_four = out_grad.reshape(tiles_here, TILE, heads_here, HEAD_DIM)

    def head_block(head_number):
        query_head = lax.dynamic_index_in_dim(query_four, head_number, 2, keepdims=False)
        grad_head = lax.dynamic_index_in_dim(grad_four, head_number, 2, keepdims=False)
        wkeys = lax.dynamic_index_in_dim(window_keys, head_number, 2, keepdims=False)
        wvals = lax.dynamic_index_in_dim(window_vals, head_number, 2, keepdims=False)
        gkeys = lax.dynamic_index_in_dim(global_keys, head_number, 1, keepdims=False)
        gvals = lax.dynamic_index_in_dim(global_vals, head_number, 1, keepdims=False)
        score_window = (
            jnp.einsum("tqd,tkd->tqk", query_head, wkeys, preferred_element_type=jnp.float32)
            * factor
        )
        score_global = (
            jnp.einsum("tqd,kd->tqk", query_head, gkeys, preferred_element_type=jnp.float32)
            * factor
        )
        score_global = jnp.where(live_mask, score_global, -jnp.inf)
        scores = jnp.concatenate([score_window, score_global], axis=2)
        largest = jnp.max(scores, axis=2, keepdims=True)
        log_total = largest + jnp.log(jnp.sum(jnp.exp(scores - largest), axis=2, keepdims=True))
        probs = jnp.exp(scores - log_total)
        probs_low = probs.astype(jnp.bfloat16)
        attended = jnp.einsum(
            "tqk,tkd->tqd", probs_low[..., :window_count], wvals, preferred_element_type=jnp.float32
        )
        attended = attended + jnp.einsum(
            "tqk,kd->tqd", probs_low[..., window_count:], gvals, preferred_element_type=jnp.float32
        )
        attended = lax.optimization_barrier(attended.astype(jnp.bfloat16))
        delta_rows = jnp.sum(grad_head.astype(jnp.float32) * attended.astype(jnp.float32), axis=2)
        dprob = jnp.concatenate(
            [
                jnp.einsum("tqd,tkd->tqk", grad_head, wvals, preferred_element_type=jnp.float32),
                jnp.einsum("tqd,kd->tqk", grad_head, gvals, preferred_element_type=jnp.float32),
            ],
            axis=2,
        )
        dscore = (probs * (dprob - delta_rows[..., None]) * factor).astype(jnp.bfloat16)
        grad_query = jnp.einsum(
            "tqk,tkd->tqd", dscore[..., :window_count], wkeys, preferred_element_type=jnp.float32
        )
        grad_query = grad_query + jnp.einsum(
            "tqk,kd->tqd", dscore[..., window_count:], gkeys, preferred_element_type=jnp.float32
        )
        window_dk = jnp.einsum(
            "tqk,tqd->tkd",
            dscore[..., :window_count],
            query_head,
            preferred_element_type=jnp.float32,
        )
        window_dv = jnp.einsum(
            "tqk,tqd->tkd",
            probs_low[..., :window_count],
            grad_head,
            preferred_element_type=jnp.float32,
        )
        global_dk = jnp.einsum(
            "tqk,tqd->kd",
            dscore[..., window_count:],
            query_head,
            preferred_element_type=jnp.float32,
        )
        global_dv = jnp.einsum(
            "tqk,tqd->kd",
            probs_low[..., window_count:],
            grad_head,
            preferred_element_type=jnp.float32,
        )
        return (grad_query, window_dk, window_dv, global_dk, global_dv)

    head_results = lax.map(head_block, jnp.arange(heads_here, dtype=jnp.int32))
    grad_query = jnp.moveaxis(head_results[0], 0, 2).reshape(tokens_here, width_here)
    window_dk = jnp.moveaxis(head_results[1], 0, 2).reshape(-1, width_here)
    window_dv = jnp.moveaxis(head_results[2], 0, 2).reshape(-1, width_here)
    global_dk = jnp.moveaxis(head_results[3], 0, 1).reshape(-1, width_here)
    global_dv = jnp.moveaxis(head_results[4], 0, 1).reshape(-1, width_here)
    window_grads = jnp.zeros((2, window_pair.shape[1], width_here), jnp.float32)
    window_grads = window_grads.at[:, window_rows.reshape(-1)].add(
        jnp.stack([window_dk, window_dv])
    )
    spread_grads = window_grads.reshape(2, 2 * REACH + 1, tokens_here, width_here)
    slots = [spread_grads[:, slot_index] for slot_index in range(2 * REACH + 1)]
    carried = slots[2 * REACH]
    for hop_index in range(2 * REACH):
        carried = (
            passed_along(carried.astype(jnp.bfloat16), "ctx", 1).astype(carried.dtype)
            + slots[2 * REACH - 1 - hop_index]
        )
    home_grads = passed_along(carried.astype(jnp.bfloat16), "ctx", -REACH).astype(carried.dtype)
    global_part = lax.psum_scatter(
        jnp.stack([global_dk, global_dv]), "ctx", scatter_dimension=1, tiled=True
    )
    home_grads = home_grads.at[:, own_rows].add(global_part)
    scaled_query = grad_query * query_gain
    scaled_key = home_grads[0] * key_gain
    query_dot, key_dot = lax.psum(
        (jnp.sum(scaled_query * query_rows, axis=1), jnp.sum(scaled_key * key_rows, axis=1)), "head"
    )
    query_grad = norm_grad(query_rows, query_inv, scaled_query, query_dot)
    key_grad = norm_grad(key_rows, key_inv, scaled_key, key_dot)
    return (query_grad, key_grad, home_grads[1].astype(jnp.bfloat16))


def solution(mesh):
    return jax.shard_map(
        body,
        mesh=mesh,
        in_specs=(
            P("ctx", "head"),
            P("ctx", "head"),
            P("ctx", "head"),
            P("ctx", "head"),
            P("head"),
            P("head"),
            P("ctx", None),
            P("ctx"),
            P("ctx", None),
        ),
        out_specs=(P("ctx", "head"), P("ctx", "head"), P("ctx", "head")),
        check_vma=False,
    )
```

profile of v0, /device:TPU:0, one launch (start us, length us, event | category | flops | bytes accessed | tf_op | source)
XLA Modules:
  0.0 1697.6 jit_solution(5765392369090235249)
XLA Ops:
  7.3 1.2 copy.58
  8.6 1.1 fusion.75
  9.7 30.9 %all-reduce.2 = (f32[256]{0:T(256)S(1)}, f32[256]{0:T(256)S(1)}) all-reduce(f32[256]{0:T(256)S(1)} %fusion.68, f32[256]{0:T(256)S(1)} %fusion.75), channel_id=1, replica_groups=mesh['ctx'=64,'head'=8] {'head'}, use_global_device_ids=true, to_apply=%region_1.0 | all-reduce | flops 512 | bytes 4096 | tf_op jit(solution)/shard_map/psum | solution.py:40
  41.2 1.1 fusion.88
  42.5 8.5 collective-permute-start
  53.0 8.4 collective-permute-done
  61.4 1.9 collective-permute-start.1
  63.4 166.6 %all_gather.3 = bf16[2,128,640]{2,0,1:T(2,128)(2,1)S(1)} all-gather(bf16[2,2,640]{2,0,1:T(2,128)(2,1)S(1)} %copy.60), channel_id=1, replica_groups=mesh['ctx'=64,'head'=8] {'ctx'}, dimensions={1}, use_global_device_ids=true | all-gather | bytes 332800 | tf_op jit(solution)/shard_map/all_gather | solution.py:47
  233.7 2.4 collective-permute-start.2
  237.4 27.7 %collective-permute-done.2 = bf16[2,256,640]{2,1,0:T(8,128)(2,1)S(1)} collective-permute-done((bf16[2,256,640]{2,1,0:T(8,128)(2,1)S(1)}, bf16[2,256,640]{2,1,0:T(8,128)(2,1)S(1)}, u32[]{:S(2)}, u32[]{:S(2)}) %collective-permute-start.2) | collective-permute-done | bytes 655392 | tf_op jit(solution)/shard_map/ppermute | solution.py:18
  265.6 5.2 gather_fusion
  270.8 4.1 reshape.218
  274.9 1.8 copy.66
  276.7 5.2 gather_fusion.3
  281.9 4.1 reshape.220
  286.0 1.8 copy.69
  287.8 76.5 %while.19 = (s32[]{:T(128)}, f32[5,2,128,128]{3,2,1,0:T(8,128)}, f32[5,2,512,128]{3,2,1,0:T(8,128)}, f32[5,2,512,128]{3,2,1,0:T(8,128)}, f32[5,128,128]{1,2,0:T(...) while((s32[]{:T(128)}, f32[5,2,128,128]{3,2,1,0:T(8,128)}, ...), condition=%wide.region_9.10_spmd.clone, body=%wide.region_4.9_spmd.clone.sunk | while | flops 254377472 | bytes 9916299 | solution.py:143
  293.3 1.0 fusion.145
  294.8 0.9 fusion.148
  297.4 1.1 fusion.153
  298.5 1.1 fusion.154
  299.6 0.9 fusion.151
  308.6 1.0 fusion.145
  310.1 0.9 fusion.148
  312.7 1.1 fusion.153
  313.8 1.1 fusion.154
  314.9 0.9 fusion.151
  323.9 1.0 fusion.145
  325.3 0.9 fusion.148
  328.0 1.1 fusion.153
  329.1 1.1 fusion.154
  330.2 0.9 fusion.151
  339.2 1.0 fusion.145
  340.6 0.9 fusion.148
  343.3 1.1 fusion.153
  344.4 1.1 fusion.154
  354.5 1.0 fusion.145
  355.9 0.9 fusion.148
  358.6 1.1 fusion.153
  359.7 1.1 fusion.154
  364.3 5.1 copy.72
  369.3 3.7 stack_reshape.12
  373.0 5.1 copy.73
  378.1 4.8 stack_reshape.13
  383.0 4.7 maximum_bitcast_fusion
  387.7 8.8 copy.74
  396.5 3.0 broadcast_in_dim.59
  399.4 131.0 %scatter_fusion = f32[2,768,640]{2,0,1:T(2,128)} fusion(f32[2,768,640]{2,0,1:T(2,128)} %broadcast_in_dim.59, s32[1024]{0:T(1024)S(1)} %bitcast.214, f32[1024,2,640]{2,1,0:T(2,128)} %copy.74), kind=kCustom, calls=%fused_computation.4 | custom fusion | flops 1310720 | bytes 15732736 | tf_op jit(solution)/shard_map/scatter-add | solution.py:150
  530.4 1.8 fusion.82
  532.3 1.9 collective-permute-start.3
  534.2 24.1 %collective-permute-done.3 = bf16[2,256,640]{2,0,1:T(2,128)(2,1)S(1)} collective-permute-done((bf16[2,256,640]{2,0,1:T(2,128)(2,1)S(1)}, bf16[2,256,640]{2,0,1:T(2,128)(2,1)S(1)}, u32[]{:S(2)}, u32[]{:S(2)}) %collective-permute-start.3) | collective-permute-done | bytes 655392 | tf_op jit(solution)/shard_map/ppermute | solution.py:18
  558.3 2.0 fusion.67
  560.4 2.1 collective-permute-start.4
  562.5 1.0 pad_maximum_fusion.2
  563.5 1.2 copy.77
  564.8 20.6 %collective-permute-done.4 = bf16[2,256,640]{2,0,1:T(2,128)(2,1)S(1)} collective-permute-done((bf16[2,256,640]{2,0,1:T(2,128)(2,1)S(1)}, bf16[2,256,640]{2,0,1:T(2,128)(2,1)S(1)}, u32[]{:S(2)}, u32[]{:S(2)}) %collective-permute-start.4) | collective-permute-done | bytes 655392 | tf_op jit(solution)/shard_map/ppermute | solution.py:18
  585.4 2.0 fusion.65
  587.4 1.9 collective-permute-start.5
  589.3 1.3 dynamic-slice
  592.3 1057.6 %all-reduce.5.cloned.1.call-done = f32[2,128,640]{2,0,1:T(2,128)} async-done(((f32[2,128,640]{2,0,1:T(2,128)}), f32[2,128,640]{2,0,1:T(2,128)}) %all-reduce.5.cloned.1.call-update) | async-done | bytes 655376
  1650.7 1.6 convert_element_type.66
  1653.4 1.5 slice.111
  1655.1 32.8 %all-reduce.1 = (f32[256]{0:T(256)S(1)}, f32[256]{0:T(256)S(1)}) all-reduce(f32[256]{0:T(256)S(1)} %fusion.74, f32[256]{0:T(256)S(1)} %fusion.81), channel_id=1, replica_groups=mesh['ctx'=64,'head'=8] {'head'}, use_global_device_ids=true, to_apply=%region_11.12 | all-reduce | flops 512 | bytes 4096 | tf_op jit(solution)/shard_map/psum | solution.py:168
  1689.8 0.9 fusion.80
  (211 shorter events, 55.7 us)
Async XLA Ops:
  7.2 45.1 %copy-start = (bf16[256,640]{1,0:T(8,128)(2,1)S(1)}, bf16[256,640]{1,0:T(8,128)(2,1)}, u32[]{:S(2)}) copy-start(bf16[256,640]{1,0:T(8,128)(2,1)} %param.12) | copy-start | bytes 983044
  7.2 45.1 %copy-start.9 = (f32[640]{0:T(1024)S(1)}, f32[640]{0:T(1024)}, u32[]{:S(2)}) copy-start(f32[640]{0:T(1024)} %param.16) | copy-start | bytes 7684
  7.2 35.2 %copy-start.6 = (bf16[256,640]{1,0:T(8,128)(2,1)S(1)}, bf16[256,640]{1,0:T(8,128)(2,1)}, u32[]{:S(2)}) copy-start(bf16[256,640]{1,0:T(8,128)(2,1)} %param.13) | copy-start | bytes 983044
  7.2 43.9 %copy-start.21 = (s32[2,4]{1,0:T(2,128)S(1)}, s32[2,4]{1,0:T(2,128)}, u32[]{:S(2)}) copy-start(s32[2,4]{1,0:T(2,128)} %param.17) | copy-start | bytes 100
  7.2 44.0 %copy-start.22 = (s32[2]{0:T(128)S(1)}, s32[2]{0:T(128)}, u32[]{:S(2)}) copy-start(s32[2]{0:T(128)} %param.18) | copy-start | bytes 28
  7.2 1642.7 %all-reduce.5.cloned.1.call-start = ((), (), s32[]{:S(2)}) async-start(), calls=%async_computation | async-start | bytes 1310720
  8.5 223.8 %copy-start.2 = (bf16[256,640]{0,1:T(8,128)(2,1)}, bf16[256,640]{0,1:T(8,128)(2,1)S(1)}, u32[]{:S(2)}) copy-start(bf16[256,640]{0,1:T(8,128)(2,1)S(1)} %copy.58) | copy-start | bytes 983044
  41.2 22.1 %copy-start.13 = (f32[256]{0:T(256)}, f32[256]{0:T(256)S(1)}, u32[]{:S(2)}) copy-start(f32[256]{0:T(256)S(1)} %get-tuple-element.204) | copy-start | bytes 3076
  41.2 191.0 %copy-start.15 = (f32[256]{0:T(256)}, f32[256]{0:T(256)S(1)}, u32[]{:S(2)}) copy-start(f32[256]{0:T(256)S(1)} %get-tuple-element.207) | copy-start | bytes 3076
  42.5 189.8 %copy-start.10 = (f32[640]{0:T(1024)S(1)}, f32[640]{0:T(1024)}, u32[]{:S(2)}) copy-start(f32[640]{0:T(1024)} %param.15) | copy-start | bytes 7684
  42.5 18.9 %collective-permute-start = (bf16[2,256,640]{2,1,0:T(8,128)(2,1)S(1)}, bf16[2,256,640]{2,1,0:T(8,128)(2,1)S(1)}, u32[]{:S(2)}, u32[]{:S(2)}) collective-permute-start(bf16[2,256,640]{2,1,0:T(8,128)(2,1)S(1)} %pad_maximum_fusion.1), channel_id=1, source_target_pairs={{0,504},{8,0},{16,8},{24,16},{32,24},{40,32},{48,40},{56,48},{64,5... | collective-permute-start | bytes 1966088 | tf_op jit(solution)/shard_map/ppermute | solution.py:18
  51.2 0.5 copy-start.19
  61.4 172.3 %collective-permute-start.1 = (bf16[2,256,640]{2,1,0:T(8,128)(2,1)S(1)}, bf16[2,256,640]{2,1,0:T(8,128)(2,1)S(1)}, u32[]{:S(2)}, u32[]{:S(2)}) collective-permute-start(bf16[2,256,640]{2,1,0:T(8,128)(2,1)S(1)} %collective-permute-done), channel_id=1, source_target_pairs={{0,8},{8,16},{16,24},{24,32},{32,40},{40,48},{48,56},{56,64},{64,7... | collective-permute-start | bytes 1966088 | tf_op jit(solution)/shard_map/ppermute | solution.py:18
  63.4 169.9 %copy-start.8 = (bf16[256,640]{1,0:T(8,128)(2,1)S(1)}, bf16[256,640]{1,0:T(8,128)(2,1)}, u32[]{:S(2)}) copy-start(bf16[256,640]{1,0:T(8,128)(2,1)} %param.14) | copy-start | bytes 983044
  230.5 5.7 copy-start.23
  233.7 31.4 %collective-permute-start.2 = (bf16[2,256,640]{2,1,0:T(8,128)(2,1)S(1)}, bf16[2,256,640]{2,1,0:T(8,128)(2,1)S(1)}, u32[]{:S(2)}, u32[]{:S(2)}) collective-permute-start(bf16[2,256,640]{2,1,0:T(8,128)(2,1)S(1)} %collective-permute-done.1), channel_id=1, source_target_pairs={{0,8},{8,16},{16,24},{24,32},{32,40},{40,48},{48,56},{56,64},{64,7... | collective-permute-start | bytes 1966088 | tf_op jit(solution)/shard_map/ppermute | solution.py:18
  287.8 4.0 copy-start.24
  297.4 5.7 copy-start.25
  303.1 4.0 copy-start.24
  312.7 5.7 copy-start.25
  318.4 4.0 copy-start.24
  328.0 5.7 copy-start.25
  333.7 4.0 copy-start.24
  343.3 5.7 copy-start.25
  349.0 4.0 copy-start.24
  358.6 5.7 copy-start.25
  396.5 3.0 copy-start.12
  530.4 32.1 %copy-start.7 = (f32[5,128,128]{1,2,0:T(8,128)S(1)}, f32[5,128,128]{1,2,0:T(8,128)}, u32[]{:S(2)}) copy-start(f32[5,128,128]{1,2,0:T(8,128)} %get-tuple-element.82) | copy-start | bytes 983044
  532.3 26.1 %collective-permute-start.3 = (bf16[2,256,640]{2,0,1:T(2,128)(2,1)S(1)}, bf16[2,256,640]{2,0,1:T(2,128)(2,1)S(1)}, u32[]{:S(2)}, u32[]{:S(2)}) collective-permute-start(bf16[2,256,640]{2,0,1:T(2,128)(2,1)S(1)} %fusion.82), channel_id=1, source_target_pairs={{0,8},{8,16},{16,24},{24,32},{32,40},{40,48},{48,56},{56,64},{64,7... | collective-permute-start | bytes 1966088 | tf_op jit(solution)/shard_map/ppermute | solution.py:18
  560.4 25.0 %collective-permute-start.4 = (bf16[2,256,640]{2,0,1:T(2,128)(2,1)S(1)}, bf16[2,256,640]{2,0,1:T(2,128)(2,1)S(1)}, u32[]{:S(2)}, u32[]{:S(2)}) collective-permute-start(bf16[2,256,640]{2,0,1:T(2,128)(2,1)S(1)} %fusion.67), channel_id=1, source_target_pairs={{0,8},{8,16},{16,24},{24,32},{32,40},{40,48},{48,56},{56,64},{64,7... | collective-permute-start | bytes 1966088 | tf_op jit(solution)/shard_map/ppermute | solution.py:18
  564.8 26.5 %copy-start.5 = (f32[5,2,128,128]{3,2,1,0:T(8,128)S(1)}, f32[5,2,128,128]{3,2,1,0:T(8,128)}, u32[]{:S(2)}) copy-start(f32[5,2,128,128]{3,2,1,0:T(8,128)} %get-tuple-element.79) | copy-start | bytes 1966084
  564.8 27.4 %copy-start.3 = (bf16[256,640]{0,1:T(8,128)(2,1)S(1)}, bf16[256,640]{0,1:T(8,128)(2,1)}, u32[]{:S(2)}) copy-start(bf16[256,640]{0,1:T(8,128)(2,1)} %copy-done.2) | copy-start | bytes 983044
  564.8 27.4 %copy-start.11 = (f32[640]{0:T(1024)S(1)}, f32[640]{0:T(1024)}, u32[]{:S(2)}) copy-start(f32[640]{0:T(1024)} %param.15) | copy-start | bytes 7684
  587.4 1063.3 %collective-permute-start.5 = (bf16[2,256,640]{2,0,1:T(2,128)(2,1)S(1)}, bf16[2,256,640]{2,0,1:T(2,128)(2,1)}, u32[]{:S(2)}, u32[]{:S(2)}) collective-permute-start(bf16[2,256,640]{2,0,1:T(2,128)(2,1)S(1)} %fusion.65), channel_id=1, source_target_pairs={{0,504},{8,0},{16,8},{24,16},{32,24},{40,32},{48,40},{56,48},{64,5... | collective-permute-start | bytes 1966088 | tf_op jit(solution)/shard_map/ppermute | solution.py:18
  591.2 1061.0 %copy-start.20 = (s32[2]{0:T(128)S(1)}, s32[2]{0:T(128)}, u32[]{:S(2)}) copy-start(s32[2]{0:T(128)} %copy-done.19) | copy-start | bytes 28
  1650.7 4.2 copy-start.1
  1652.3 35.7 %copy-start.16 = (f32[256]{0:T(256)S(1)}, f32[256]{0:T(256)}, u32[]{:S(2)}) copy-start(f32[256]{0:T(256)} %copy-done.15) | copy-start | bytes 3076
  1652.3 35.7 %copy-start.18 = (f32[256]{0:T(256)S(1)}, f32[256]{0:T(256)}, u32[]{:S(2)}) copy-start(f32[256]{0:T(256)} %get-tuple-element.208) | copy-start | bytes 3076
  1654.9 34.1 %copy-start.4 = (bf16[1,256,640]{2,0,1:T(2,128)(2,1)S(1)}, bf16[1,256,640]{2,0,1:T(2,128)(2,1)}, u32[]{:S(2)}) copy-start(bf16[1,256,640]{2,0,1:T(2,128)(2,1)} %slice.111) | copy-start | bytes 983044
  1654.9 34.9 %copy-start.14 = (f32[256]{0:T(256)S(1)}, f32[256]{0:T(256)}, u32[]{:S(2)}) copy-start(f32[256]{0:T(256)} %copy-done.13) | copy-start | bytes 3076
  1654.9 34.9 %copy-start.17 = (f32[256]{0:T(256)S(1)}, f32[256]{0:T(256)}, u32[]{:S(2)}) copy-start(f32[256]{0:T(256)} %get-tuple-element.203) | copy-start | bytes 3076
Sparse Core Ops, SparseCore 0:
  564.9 1085.0 all-reduce.4
where the time goes:
time: 1700 us
  waiting for transfers between devices  1140 us (67%)
  blocking collectives  230 us (14%)
  other arithmetic  153 us (9%)
  local copies, waits for them, and re-layouts  84.9 us (5%)
  matrix products  46.1 us (3%)
  starting transfers between devices  18.9 us (1%)
    unnamed x2, waiting for transfers between devices  1060 us
    all_gather x1, blocking collectives, body(): global_pair = lax.all_gather(own_pair, 'ctx', axis=1, tiled=True)  167 us
    scatter-add x1, other arithmetic, body(): window_grads.at[:, window_rows.reshape(-1)]  131 us
    ppermute x6, waiting for transfers between devices, passed_along(): lax.ppermute(shard, axis, [(i, (i + by) % count) for i in range(count)])  80.8 us
  transfers between devices with their start and end apart: 7, of which 5 were waited for; matrix products, arithmetic and copies ran while one was open for 1% of the time, Pallas kernels for 0%

commit v1 on v0

v1 whole, which is shorter than its diff:
```python
import functools

import jax
import jax.numpy as jnp
from jax import lax
from jax.experimental import pallas as pl
from jax.experimental.pallas import tpu as pltpu
from jax.sharding import PartitionSpec as P

HEAD_DIM = 128
D = 5120
TILE = 128
KEYS = 4
G_DEV = 2
MESH = pl.DeviceIdType.MESH

LOW = 8
ZN = 2

EPSILON = 1e-06


def normalize(as_float, gain, squares):
    inverse = lax.rsqrt(squares[:, None] / D + EPSILON)
    return (inverse, (as_float * inverse * gain).astype(jnp.bfloat16))


def norm_grad(as_float, inverse, scaled, coeffs):
    return (inverse * scaled - as_float * inverse**3 * (coeffs[:, None] / D)).astype(jnp.bfloat16)


def greet(targets):
    barrier = pltpu.get_barrier_semaphore()
    for target in targets:
        pl.semaphore_signal(barrier, inc=1, device_id=target, device_id_type=MESH)
    pl.semaphore_wait(barrier, len(targets))


def head_sum_kernel(count, x_ref, o_ref, slots, send_sem, recv_sem):
    me = lax.axis_index("head")
    peers = [{"head": lax.rem(me + o, count)} for o in range(1, count)]
    greet(peers)
    copies = []
    for o, peer in enumerate(peers):
        copy = pltpu.make_async_remote_copy(
            src_ref=x_ref,
            dst_ref=slots.at[o],
            send_sem=send_sem.at[o],
            recv_sem=recv_sem.at[o],
            device_id=peer,
            device_id_type=MESH,
        )
        copy.start()
        copies.append(copy)
    total = x_ref[...]
    for o, copy in enumerate(copies):
        copy.wait_recv()
        total = total + slots[o]
    o_ref[...] = total
    for copy in copies:
        copy.wait_send()


def head_sum(pair, collective_id):
    count = lax.axis_size("head")
    flat = pair.reshape(-1, 128)
    out = pl.pallas_call(
        functools.partial(head_sum_kernel, count),
        out_shape=jax.ShapeDtypeStruct(flat.shape, jnp.float32),
        in_specs=[pl.BlockSpec(memory_space=pltpu.VMEM)],
        out_specs=pl.BlockSpec(memory_space=pltpu.VMEM),
        scratch_shapes=[
            pltpu.VMEM((count - 1,) + flat.shape, jnp.float32),
            pltpu.SemaphoreType.DMA((count - 1,)),
            pltpu.SemaphoreType.DMA((count - 1,)),
        ],
        compiler_params=pltpu.CompilerParams(collective_id=collective_id, has_side_effects=True),
    )(flat)
    return out.reshape(pair.shape)


def places(count):
    me = lax.axis_index("ctx")
    yn = count // (LOW * ZN)
    low = lax.rem(me, LOW)
    z = lax.rem(me // LOW, ZN)
    y = me // (LOW * ZN)

    def at(y, z, low):
        return {"ctx": (y * ZN + z) * LOW + low}

    other_z = at(y, 1 - z, low)
    y_peers = [at(lax.rem(y + o, yn), z, low) for o in range(1, yn)]
    low_peers = [at(y, z, lax.rem(low + o, LOW)) for o in range(1, LOW)]
    after = {"ctx": lax.rem(me + 1, count)}
    before = {"ctx": lax.rem(me + count - 1, count)}
    return y, z, low, yn, other_z, y_peers, low_peers, after, before


def spread_kernel(count, kv_ref, own_ref, win_ref, glob_ref, wsend, wrecv, gsend, grecv, lsem):
    y, z, low, yn, other_z, y_peers, low_peers, after, before = places(count)
    greet([after, before, other_z] + y_peers + low_peers)

    def remote(src, dst, send_sem, recv_sem, target):
        return pltpu.make_async_remote_copy(
            src_ref=src,
            dst_ref=dst,
            send_sem=send_sem,
            recv_sem=recv_sem,
            device_id=target,
            device_id_type=MESH,
        )

    swap = remote(own_ref, glob_ref.at[low, y, z], gsend.at[0], grecv.at[0], other_z)
    swap.start()
    up = remote(kv_ref, win_ref.at[0], wsend.at[0], wrecv.at[0], after)
    down = remote(kv_ref, win_ref.at[1], wsend.at[1], wrecv.at[1], before)
    up.start()
    down.start()
    local = pltpu.make_async_copy(own_ref, glob_ref.at[low, y, z], lsem)
    local.start()
    local.wait()
    remote(own_ref, glob_ref.at[low, y, 1 - z], gsend.at[0], grecv.at[0], other_z).wait_recv()
    sent = [swap]
    for o, peer in enumerate(y_peers):
        copy = remote(glob_ref.at[low, y], glob_ref.at[low, y], gsend.at[1 + o], grecv.at[1 + o], peer)
        copy.start()
        sent.append(copy)
    for o, peer in enumerate(y_peers):
        source = lax.rem(y + yn - 1 - o, yn)
        remote(
            glob_ref.at[low, source], glob_ref.at[low, source], gsend.at[1 + o], grecv.at[1 + o], peer
        ).wait_recv()
    for o, peer in enumerate(low_peers):
        copy = remote(glob_ref.at[low], glob_ref.at[low], gsend.at[yn + o], grecv.at[yn + o], peer)
        copy.start()
        sent.append(copy)
    for o, peer in enumerate(low_peers):
        source = lax.rem(low + LOW - 1 - o, LOW)
        remote(
            glob_ref.at[source], glob_ref.at[source], gsend.at[yn + o], grecv.at[yn + o], peer
        ).wait_recv()
    up.wait()
    down.wait()
    for copy in sent:
        copy.wait_send()


def spread(key_value, own_rows):
    count = lax.axis_size("ctx")
    yn = count // (LOW * ZN)
    width = own_rows.shape[-1]
    copies = yn + LOW - 1
    return pl.pallas_call(
        functools.partial(spread_kernel, count),
        out_shape=(
            jax.ShapeDtypeStruct((2,) + key_value.shape, jnp.bfloat16),
            jax.ShapeDtypeStruct((LOW, yn, ZN, 2 * G_DEV, width), jnp.bfloat16),
        ),
        in_specs=[pl.BlockSpec(memory_space=pl.ANY)] * 2,
        out_specs=(pl.BlockSpec(memory_space=pl.ANY),) * 2,
        scratch_shapes=[
            pltpu.SemaphoreType.DMA((2,)),
            pltpu.SemaphoreType.DMA((2,)),
            pltpu.SemaphoreType.DMA((copies,)),
            pltpu.SemaphoreType.DMA((copies,)),
            pltpu.SemaphoreType.DMA,
        ],
        compiler_params=pltpu.CompilerParams(collective_id=1, has_side_effects=True),
    )(key_value, own_rows)


def collect_kernel(
    count, prev_ref, next_ref, part_ref, from_ref, sum_ref,
    slots, half, yslots, quarter, zslot, wsend, wrecv, gsend, grecv,
):
    y, z, low, yn, other_z, y_peers, low_peers, after, before = places(count)
    greet([after, before, other_z] + y_peers + low_peers)

    def remote(src, dst, send_sem, recv_sem, target):
        return pltpu.make_async_remote_copy(
            src_ref=src,
            dst_ref=dst,
            send_sem=send_sem,
            recv_sem=recv_sem,
            device_id=target,
            device_id_type=MESH,
        )

    sent = []
    for o, peer in enumerate(low_peers):
        copy = remote(
            part_ref.at[lax.rem(low + 1 + o, LOW)], slots.at[o], gsend.at[o], grecv.at[o], peer
        )
        copy.start()
        sent.append(copy)
    up = remote(next_ref, from_ref.at[0], wsend.at[0], wrecv.at[0], after)
    down = remote(prev_ref, from_ref.at[1], wsend.at[1], wrecv.at[1], before)
    up.start()
    down.start()
    total = part_ref[low]
    for o, copy in enumerate(sent):
        copy.wait_recv()
        total = total + slots[o]
    half[...] = total
    ysent = []
    for o, peer in enumerate(y_peers):
        index = LOW - 1 + o
        copy = remote(
            half.at[lax.rem(y + 1 + o, yn)], yslots.at[o], gsend.at[index], grecv.at[index], peer
        )
        copy.start()
        ysent.append(copy)
    row = half[y]
    for o, copy in enumerate(ysent):
        copy.wait_recv()
        row = row + yslots[o]
    quarter[...] = row
    last = LOW - 1 + yn - 1
    swap = remote(quarter, zslot, gsend.at[last], grecv.at[last], other_z)
    swap.start()
    swap.wait_recv()
    sum_ref[...] = row + zslot[...]
    for copy in sent + ysent + [swap]:
        copy.wait_send()
    up.wait()
    down.wait()


def collect(to_prev, to_next, parts):
    count = lax.axis_size("ctx")
    yn = count // (LOW * ZN)
    rows, width = parts.shape[2:]
    copies = LOW - 1 + yn
    return pl.pallas_call(
        functools.partial(collect_kernel, count),
        out_shape=(
            jax.ShapeDtypeStruct((2,) + to_prev.shape, jnp.bfloat16),
            jax.ShapeDtypeStruct((rows, width), jnp.float32),
        ),
        in_specs=[
            pl.BlockSpec(memory_space=pl.ANY),
            pl.BlockSpec(memory_space=pl.ANY),
            pl.BlockSpec(memory_space=pltpu.VMEM),
        ],
        out_specs=(pl.BlockSpec(memory_space=pl.ANY), pl.BlockSpec(memory_space=pltpu.VMEM)),
        scratch_shapes=[
            pltpu.VMEM((LOW - 1, yn, rows, width), jnp.float32),
            pltpu.VMEM((yn, rows, width), jnp.float32),
            pltpu.VMEM((yn - 1, rows, width), jnp.float32),
            pltpu.VMEM((rows, width), jnp.float32),
            pltpu.VMEM((rows, width), jnp.float32),
            pltpu.SemaphoreType.DMA((2,)),
            pltpu.SemaphoreType.DMA((2,)),
            pltpu.SemaphoreType.DMA((copies,)),
            pltpu.SemaphoreType.DMA((copies,)),
        ],
        compiler_params=pltpu.CompilerParams(collective_id=2, has_side_effects=True),
    )(to_prev, to_next, parts)


def dot(a, b, dims):
    return lax.dot_general(a, b, (dims, ((), ())), preferred_element_type=jnp.float32)


ROWS = ((1,), (0,))
TURNED = ((1,), (1,))
DOWN = ((0,), (0,))


def attention_kernel(
    start_ref, live_ref, q_ref, g_ref, kv_ref, win_ref, glob_ref,
    dq_ref, prev_ref, next_ref, own_ref, dglob_ref, keys, vals, dkeys, dvals,
):
    tokens = q_ref.shape[0]
    span = KEYS * TILE
    factor = HEAD_DIM ** (-0.5)
    for pair_index, cat in enumerate((keys, vals)):
        cat[0:tokens] = win_ref[0, pair_index]
        cat[tokens : 2 * tokens] = kv_ref[pair_index]
        cat[2 * tokens :] = win_ref[1, pair_index]
    dkeys[...] = jnp.zeros_like(dkeys)
    dvals[...] = jnp.zeros_like(dvals)
    gkeys = glob_ref[0]
    gvals = glob_ref[1]
    live = live_ref[...] > 0
    gdk = 0.0
    gdv = 0.0
    for tile in range(tokens // TILE):
        rows = slice(tile * TILE, (tile + 1) * TILE)
        window = pl.ds(pl.multiple_of(start_ref[tile] * TILE, TILE), span)
        query = q_ref[rows]
        grad = g_ref[rows]
        wkeys = keys[window]
        wvals = vals[window]
        score_w = dot(query, wkeys, TURNED) * factor
        score_g = jnp.where(live, dot(query, gkeys, TURNED) * factor, -jnp.inf)
        largest = jnp.maximum(
            jnp.max(score_w, axis=1, keepdims=True), jnp.max(score_g, axis=1, keepdims=True)
        )
        exp_w = jnp.exp(score_w - largest)
        exp_g = jnp.exp(score_g - largest)
        inverse = 1.0 / (
            jnp.sum(exp_w, axis=1, keepdims=True) + jnp.sum(exp_g, axis=1, keepdims=True)
        )
        prob_w = exp_w * inverse
        prob_g = exp_g * inverse
        low_w = prob_w.astype(jnp.bfloat16)
        low_g = prob_g.astype(jnp.bfloat16)
        attended = (dot(low_w, wvals, ROWS) + dot(low_g, gvals, ROWS)).astype(jnp.bfloat16)
        delta = jnp.sum(
            grad.astype(jnp.float32) * attended.astype(jnp.float32), axis=1, keepdims=True
        )
        ds_w = (prob_w * (dot(grad, wvals, TURNED) - delta) * factor).astype(jnp.bfloat16)
        ds_g = (prob_g * (dot(grad, gvals, TURNED) - delta) * factor).astype(jnp.bfloat16)
        dq_ref[rows] = dot(ds_w, wkeys, ROWS) + dot(ds_g, gkeys, ROWS)
        dkeys[window] += dot(ds_w, query, DOWN)
        dvals[window] += dot(low_w, grad, DOWN)
        gdk = gdk + dot(ds_g, query, DOWN)
        gdv = gdv + dot(low_g, grad, DOWN)
    for pair_index, cat in enumerate((dkeys, dvals)):
        prev_ref[pair_index] = cat[0:tokens].astype(jnp.bfloat16)
        own_ref[pair_index] = cat[tokens : 2 * tokens]
        next_ref[pair_index] = cat[2 * tokens :].astype(jnp.bfloat16)
    dglob_ref[0] = gdk
    dglob_ref[1] = gdv


def attention(starts, live, query_norm, out_grad, key_value, window, globs):
    tokens, width = query_norm.shape
    count = globs.shape[1]
    flat = pl.BlockSpec((tokens, HEAD_DIM), lambda h: (0, h))
    pair = pl.BlockSpec((2, tokens, HEAD_DIM), lambda h: (0, 0, h))
    glob = pl.BlockSpec((2, count, HEAD_DIM), lambda h: (0, 0, h))
    pair_shape = (2, tokens, width)
    return pl.pallas_call(
        attention_kernel,
        grid=(width // HEAD_DIM,),
        out_shape=(
            jax.ShapeDtypeStruct((tokens, width), jnp.float32),
            jax.ShapeDtypeStruct(pair_shape, jnp.bfloat16),
            jax.ShapeDtypeStruct(pair_shape, jnp.bfloat16),
            jax.ShapeDtypeStruct(pair_shape, jnp.float32),
            jax.ShapeDtypeStruct((2, count, width), jnp.float32),
        ),
        in_specs=[
            pl.BlockSpec(memory_space=pltpu.SMEM),
            pl.BlockSpec(memory_space=pltpu.VMEM),
            flat,
            flat,
            pair,
            pl.BlockSpec((2, 2, tokens, HEAD_DIM), lambda h: (0, 0, 0, h)),
            glob,
        ],
        out_specs=(flat, pair, pair, pair, glob),
        scratch_shapes=[
            pltpu.VMEM((3 * tokens, HEAD_DIM), jnp.bfloat16),
            pltpu.VMEM((3 * tokens, HEAD_DIM), jnp.bfloat16),
            pltpu.VMEM((3 * tokens, HEAD_DIM), jnp.float32),
            pltpu.VMEM((3 * tokens, HEAD_DIM), jnp.float32),
        ],
    )(starts, live, query_norm, out_grad, key_value, window, globs)


def body(
    query_raw, key_raw, values, out_grad, query_gain, key_gain, key_tiles, global_ids, readers
):
    tokens_here, width = query_raw.shape
    tiles_here = tokens_here // TILE
    count = lax.axis_size("ctx")
    yn = count // (LOW * ZN)
    device = lax.axis_index("ctx")
    query_rows = query_raw.astype(jnp.float32)
    key_rows = key_raw.astype(jnp.float32)
    squares = head_sum(
        jnp.stack([jnp.sum(query_rows * query_rows, axis=1), jnp.sum(key_rows * key_rows, axis=1)]),
        0,
    )
    query_inv, query_norm = normalize(query_rows, query_gain, squares[0])
    key_inv, key_norm = normalize(key_rows, key_gain, squares[1])
    key_value = jnp.stack([key_norm, values])
    own_rows = global_ids - device * tokens_here
    own_pair = key_value[:, own_rows].reshape(2 * G_DEV, width)
    window, globs = spread(key_value, own_pair)
    globs = (
        globs.reshape(LOW, yn, ZN, 2, G_DEV, width)
        .transpose(3, 1, 2, 0, 4, 5)
        .reshape(2, count * G_DEV, width)
    )
    live = jnp.repeat(readers, G_DEV, axis=1)
    starts = jnp.clip(key_tiles[:, 0] - (device - 1) * tiles_here, 0, 3 * tiles_here - KEYS)
    grad_query, to_prev, to_next, own_grads, glob_grads = attention(
        starts, live, query_norm, out_grad, key_value, window, globs
    )
    parts = (
        glob_grads.reshape(2, yn, ZN, LOW, G_DEV, width)
        .transpose(3, 1, 2, 0, 4, 5)
        .reshape(LOW, yn, ZN * 2 * G_DEV, width)
    )
    arrived, reduced = collect(to_prev, to_next, parts)
    mine = lax.dynamic_index_in_dim(
        reduced.reshape(ZN, 2, G_DEV, width), lax.rem(device // LOW, ZN), 0, keepdims=False
    )
    home = own_grads + arrived[0].astype(jnp.float32) + arrived[1].astype(jnp.float32)
    spots = jnp.arange(tokens_here, dtype=jnp.int32)[:, None]
    for index in range(G_DEV):
        home = home + jnp.where(spots == own_rows[index], mine[:, index][:, None, :], 0.0)
    scaled_query = grad_query * query_gain
    scaled_key = home[0] * key_gain
    dots = head_sum(
        jnp.stack([jnp.sum(scaled_query * query_rows, axis=1), jnp.sum(scaled_key * key_rows, axis=1)]),
        3,
    )
    query_grad = norm_grad(query_rows, query_inv, scaled_query, dots[0])
    key_grad = norm_grad(key_rows, key_inv, scaled_key, dots[1])
    return (query_grad, key_grad, home[1].astype(jnp.bfloat16))


def solution(mesh):
    return jax.shard_map(
        body,
        mesh=mesh,
        in_specs=(
            P("ctx", "head"),
            P("ctx", "head"),
            P("ctx", "head"),
            P("ctx", "head"),
            P("head"),
            P("head"),
            P("ctx", None),
            P("ctx"),
            P("ctx", None),
        ),
        out_specs=(P("ctx", "head"), P("ctx", "head"), P("ctx", "head")),
        check_vma=False,
    )
```

time: 1700 us -> 156 us (0.09)
  the two profiles are of different devices: /device:TPU:0 before, /device:TPU:32 now
where the time goes in v1:
time: 156 us; the launch traced here: 155 us
  Pallas kernels  131 us (84%)
  local copies, waits for them, and re-layouts  11.9 us (8%)
  other arithmetic  11.7 us (8%)
    pallas_call x1, Pallas kernels, spread(): pl.pallas_call(functools.partial(spread_kernel, count), out_shape=(jax.Sh...  46 us
    pallas_call x1, Pallas kernels, collect(): pl.pallas_call(functools.partial(collect_kernel, count), out_shape=(jax.S...  46 us
    pallas_call x2, Pallas kernels, head_sum(): pl.pallas_call(functools.partial(head_sum_kernel, count), out_shape=jax.S...  27.7 us
    pallas_call x1, Pallas kernels, attention(): pl.pallas_call(attention_kernel, grid=(width // HEAD_DIM,), out_shape=(ja...  10.9 us

profile of v1, /device:TPU:32, one launch (start us, length us, event | category | flops | bytes accessed | tf_op | source)
XLA Modules:
  0.0 155.2 jit_solution(8591117355435714782)
XLA Ops:
  0.6 0.0 copy-start.5
  0.6 0.7 compare_select_fusion
  1.4 1.1 fusion.2
  2.5 1.1 fusion.9
  3.6 0.6 reshape.129.x_ref
  4.2 16.3 %shard_map.115 = f32[4,128]{1,0:T(4,128)} custom-call(f32[4,128]{1,0:T(4,128)} %reshape.129.x_ref), custom_call_target="tpu_custom_call" | custom-call | tf_op jit(solution)/shard_map/pallas_call | solution.py:67
  20.5 0.8 rsqrt_bitcast_fusion
  21.3 1.1 fusion.18
  22.4 0.0 copy-done.5
  22.4 0.1 pad_maximum_fusion.kv_ref
  22.5 0.0 copy-start
  22.5 0.7 copy.14
  23.2 0.6 gather_fusion
  23.8 0.6 reshape.130.own_ref
  24.4 0.0 copy-done
  24.4 0.0 copy-start.9
  24.4 0.0 copy-start.1
  24.4 0.0 copy-start.6
  24.4 46.0 %shard_map.116 = (bf16[2,2,256,640]{3,2,1,0:T(8,128)(2,1)}, bf16[8,4,2,4,640]{4,3,2,1,0:T(4,128)(2,1)}) custom-call(bf16[2,256,640]{2,1,0:T(8,128)(2,1)} %copy-done, bf16[4,640]{1,0:T(4,128)(2,1)} %reshape.130.own_ref), custom_call_target="tpu_custom_call" | custom-call | tf_op jit(solution)/shard_map/pallas_call | solution.py:154
  70.4 0.0 copy-start.10
  70.4 1.1 reshape.131
  71.5 0.2 copy.25
  71.8 0.8 reshape.132.glob_ref
  72.6 0.0 copy-done.9
  72.6 0.6 clamp_reduce_fusion.start_ref
  73.3 0.0 copy-done.1
  73.3 0.0 copy-done.6
  73.3 0.9 fusion.4.q_ref
  74.1 0.0 copy-done.10
  74.1 0.1 broadcast_in_dim.48
  74.2 0.7 broadcast_in_dim.49.live_ref
  74.9 10.9 %shard_map.117 = (f32[256,640]{1,0:T(8,128)}, bf16[2,256,640]{2,1,0:T(8,128)(2,1)}, bf16[2,256,640]{2,1,0:T(8,128)(2,1)}, f32[2,256,640]{2,1,0:T(8,128)}, f32[2,128,640]{2,1,0:T(8,128)}) custom-call(s32[2]{0:T(128)} %clamp_reduce_fusion.start_ref, s32[1,128]{1,0:T(1,128)} %broadcast_in_dim.49.live_ref, bf16[256,640]{1,0:T(8,128)(2,1)} %fusion.4.q_ref, ...), custom_call_target="tpu_custom_call" | custom-call | tf_op jit(solution)/shard_map/pallas_call | solution.py:336
  85.7 1.5 reshape.133
  87.2 0.1 copy.24
  87.3 1.3 reshape.134.part_ref
  88.6 0.0 copy-start.4
  88.6 46.0 %shard_map.118 = (bf16[2,2,256,640]{3,2,1,0:T(8,128)(2,1)}, f32[8,640]{1,0:T(8,128)}) custom-call(bf16[2,256,640]{2,1,0:T(8,128)(2,1)} %get-tuple-element.16.prev_ref, bf16[2,256,640]{2,1,0:T(8,128)(2,1)} %get-tuple-element.17.next_ref, f32[8,4,8,640]{3,2,1,0:T(8,128)} %reshape.134.part_ref), custom_call_target="tpu_custom_call" | custom-call | tf_op jit(solution)/shard_map/pallas_call | solution.py:235
  134.6 0.7 reshape.135
  135.4 0.6 fusion.20
  136.0 0.6 iota_compare_fusion
  136.7 0.7 iota_compare_fusion.1
  137.3 0.0 copy-done.4
  137.4 0.0 copy-start.2
  137.4 0.0 copy-start.7
  137.4 1.7 %fusion.1 = f32[2,256,640]{2,1,0:T(8,128)S(1)} fusion(f32[2,256,640]{2,1,0:T(8,128)S(1)} %copy-done.4, f32[2,640]{1,0:T(2,128)S(1)} %bitcast.56, f32[2,640]{1,0:T(2,128)S(1)} %bitcast.57, bf16[2,2,256,640]{3,2,1,0:T(8,128)(2,1)} %get-tuple-element.19, pred[256]{0:T(512)(128)(4,1)S(1)} %iota_compare_fusion, pred[256]{0:T(512)(128)(4,1)S(1)} %iota_compare_fusion.1), kind=kLoop, calls=%fused_computation.3 | loop fusion | flops 2621440 | bytes 3942912 | tf_op jit(solution)/shard_map/add | solution.py:407
  139.1 0.0 copy-done.2
  139.1 0.0 copy-done.7
  139.1 0.0 copy-start.3
  139.1 0.0 copy-start.8
  139.1 0.2 fusion.12
  139.3 0.9 copy-done.3
  140.2 0.2 fusion.8
  140.4 0.6 reshape.136.x_ref
  141.0 11.4 %shard_map.119 = f32[4,128]{1,0:T(4,128)} custom-call(f32[4,128]{1,0:T(4,128)} %reshape.136.x_ref), custom_call_target="tpu_custom_call" | custom-call | tf_op jit(solution)/shard_map/pallas_call | solution.py:67
  152.4 0.8 multiply_bitcast_fusion
  153.2 0.0 copy-done.8
  153.2 1.2 fusion.7
  154.4 0.8 fusion.17
  (9 shorter events, 0.1 us)
Async XLA Ops:
  0.6 21.8 %copy-start.5 = (bf16[256,640]{1,0:T(8,128)(2,1)S(1)}, bf16[256,640]{1,0:T(8,128)(2,1)}, u32[]{:S(2)}) copy-start(bf16[256,640]{1,0:T(8,128)(2,1)} %param.11) | copy-start | bytes 983044
  22.5 1.9 %copy-start = (bf16[2,256,640]{2,1,0:T(8,128)(2,1)}, bf16[2,256,640]{2,1,0:T(8,128)(2,1)S(1)}, u32[]{:S(2)}) copy-start(bf16[2,256,640]{2,1,0:T(8,128)(2,1)S(1)} %pad_maximum_fusion.kv_ref) | copy-start | bytes 1966084
  24.4 48.3 %copy-start.9 = (s32[2,4]{1,0:T(2,128)S(1)}, s32[2,4]{1,0:T(2,128)}, u32[]{:S(2)}) copy-start(s32[2,4]{1,0:T(2,128)} %param.15) | copy-start | bytes 100
  24.4 48.9 %copy-start.1 = (bf16[256,640]{1,0:T(8,128)(2,1)S(1)}, bf16[256,640]{1,0:T(8,128)(2,1)}, u32[]{:S(2)}) copy-start(bf16[256,640]{1,0:T(8,128)(2,1)} %param.9) | copy-start | bytes 983044
  24.4 48.9 %copy-start.6 = (f32[640]{0:T(1024)S(1)}, f32[640]{0:T(1024)}, u32[]{:S(2)}) copy-start(f32[640]{0:T(1024)} %param.13) | copy-start | bytes 7684
  70.4 3.7 %copy-start.10 = (s32[1,64]{1,0:T(1,128)S(1)}, s32[1,64]{1,0:T(1,128)}, u32[]{:S(2)}) copy-start(s32[1,64]{1,0:T(1,128)} %param.17) | copy-start | bytes 772
  88.6 48.7 %copy-start.4 = (f32[2,256,640]{2,1,0:T(8,128)S(1)}, f32[2,256,640]{2,1,0:T(8,128)}, u32[]{:S(2)}) copy-start(f32[2,256,640]{2,1,0:T(8,128)} %get-tuple-element.15) | copy-start | bytes 3932164
  137.4 1.8 %copy-start.2 = (bf16[256,640]{1,0:T(8,128)(2,1)S(1)}, bf16[256,640]{1,0:T(8,128)(2,1)}, u32[]{:S(2)}) copy-start(bf16[256,640]{1,0:T(8,128)(2,1)} %param.10) | copy-start | bytes 983044
  137.4 1.8 %copy-start.7 = (f32[640]{0:T(1024)S(1)}, f32[640]{0:T(1024)}, u32[]{:S(2)}) copy-start(f32[640]{0:T(1024)} %param.14) | copy-start | bytes 7684
  139.1 1.1 copy-start.3
  139.1 14.1 %copy-start.8 = (f32[4,128]{1,0:T(4,128)S(1)}, f32[4,128]{1,0:T(4,128)}, u32[]{:S(2)}) copy-start(f32[4,128]{1,0:T(4,128)} %shard_map.115) | copy-start | bytes 6148

commit v2 on v1

v2 whole, which is shorter than its diff:
```python
import functools

import jax
import jax.numpy as jnp
from jax import lax
from jax.experimental import pallas as pl
from jax.experimental.pallas import tpu as pltpu
from jax.sharding import PartitionSpec as P

HEAD_DIM = 128
D = 5120
TILE = 128
KEYS = 4
G_DEV = 2
MESH = pl.DeviceIdType.MESH

LOW = 8
ZN = 2

EPSILON = 1e-06


def norm_grad(as_float, inverse, scaled, coeffs):
    return (inverse * scaled - as_float * inverse**3 * (coeffs[:, None] / D)).astype(jnp.bfloat16)


def greet(targets):
    barrier = pltpu.get_barrier_semaphore()
    for target in targets:
        pl.semaphore_signal(barrier, inc=1, device_id=target, device_id_type=MESH)
    pl.semaphore_wait(barrier, len(targets))


def remote(src, dst, sems, index, target):
    return pltpu.make_async_remote_copy(
        src_ref=src,
        dst_ref=dst,
        send_sem=sems[0].at[index],
        recv_sem=sems[1].at[index],
        device_id=target,
        device_id_type=MESH,
    )


def head_peers(heads):
    me = lax.axis_index("head")
    return [{"head": lax.rem(me + o, heads)} for o in range(1, heads)]


def start_all(src, slots, sems, peers):
    copies = [remote(src, slots.at[o], sems, o, peer) for o, peer in enumerate(peers)]
    for copy in copies:
        copy.start()
    return copies


def add_arrivals(total, slots, copies):
    for o, copy in enumerate(copies):
        copy.wait_recv()
        total = total + slots[o]
    return total


def places(count):
    me = lax.axis_index("ctx")
    yn = count // (LOW * ZN)
    low = lax.rem(me, LOW)
    z = lax.rem(me // LOW, ZN)
    y = me // (LOW * ZN)

    def at(y, z, low):
        return {"ctx": (y * ZN + z) * LOW + low}

    other_z = at(y, 1 - z, low)
    y_peers = [at(lax.rem(y + o, yn), z, low) for o in range(1, yn)]
    low_peers = [at(y, z, lax.rem(low + o, LOW)) for o in range(1, LOW)]
    after = {"ctx": lax.rem(me + 1, count)}
    before = {"ctx": lax.rem(me + count - 1, count)}
    return y, z, low, yn, other_z, y_peers, low_peers, after, before


def spread_kernel(
    count, heads, key_ref, val_ref, sq_ref, raw_ref, gain_ref,
    win_ref, glob_ref, tot_ref, near_ref,
    hslots, total_buf, near_buf, own_buf, wsend, wrecv, hsend, hrecv, gsend, grecv, lsem,
):
    y, z, low, yn, other_z, y_peers, low_peers, after, before = places(count)
    peers = head_peers(heads)
    greet(peers + [after, before, other_z] + y_peers + low_peers)
    wsems, hsems, gsems = (wsend, wrecv), (hsend, hrecv), (gsend, grecv)
    summed = start_all(sq_ref, hslots, hsems, peers)
    moved = [
        remote(key_ref, win_ref.at[0, 0], wsems, 0, after),
        remote(key_ref, win_ref.at[1, 0], wsems, 1, before),
    ]
    for copy in moved:
        copy.start()
    total = add_arrivals(sq_ref[...], hslots, summed)
    total_buf[...] = total
    tot_ref[...] = total
    raw = raw_ref[...]
    inverse = lax.rsqrt(total[4:8, 0:1] / D + EPSILON)
    is_key = lax.broadcasted_iota(jnp.int32, raw.shape, 0) < G_DEV
    own_buf[...] = jnp.where(is_key, raw * inverse * gain_ref[...], raw).astype(jnp.bfloat16)
    swap = remote(own_buf, glob_ref.at[low, y, z], gsems, 0, other_z)
    swap.start()
    local = pltpu.make_async_copy(own_buf, glob_ref.at[low, y, z], lsem)
    local.start()
    near = [
        remote(total_buf, near_buf.at[0], wsems, 4, after),
        remote(total_buf, near_buf.at[1], wsems, 5, before),
    ]
    for copy in near:
        copy.start()
    local.wait()
    remote(own_buf, glob_ref.at[low, y, 1 - z], gsems, 0, other_z).wait_recv()
    sent = [swap]
    for o, peer in enumerate(y_peers):
        copy = remote(glob_ref.at[low, y], glob_ref.at[low, y], gsems, 1 + o, peer)
        copy.start()
        sent.append(copy)
    for o, peer in enumerate(y_peers):
        source = lax.rem(y + yn - 1 - o, yn)
        remote(glob_ref.at[low, source], glob_ref.at[low, source], gsems, 1 + o, peer).wait_recv()
    for o, peer in enumerate(low_peers):
        copy = remote(glob_ref.at[low], glob_ref.at[low], gsems, yn + o, peer)
        copy.start()
        sent.append(copy)
    late = [
        remote(val_ref, win_ref.at[0, 1], wsems, 2, after),
        remote(val_ref, win_ref.at[1, 1], wsems, 3, before),
    ]
    for copy in late:
        copy.start()
    for o, peer in enumerate(low_peers):
        source = lax.rem(low + LOW - 1 - o, LOW)
        remote(glob_ref.at[source], glob_ref.at[source], gsems, yn + o, peer).wait_recv()
    for copy in near:
        copy.wait()
    near_ref[...] = near_buf[...]
    for copy in moved + late:
        copy.wait()
    for copy in sent + summed:
        copy.wait_send()


def spread(key_raw, values, squares, own_raw, gain):
    count = lax.axis_size("ctx")
    heads = lax.axis_size("head")
    yn = count // (LOW * ZN)
    width = own_raw.shape[-1]
    copies = yn + LOW - 1
    vmem = pl.BlockSpec(memory_space=pltpu.VMEM)
    free = pl.BlockSpec(memory_space=pl.ANY)
    return pl.pallas_call(
        functools.partial(spread_kernel, count, heads),
        out_shape=(
            jax.ShapeDtypeStruct((2, 2) + key_raw.shape, jnp.bfloat16),
            jax.ShapeDtypeStruct((LOW, yn, ZN, 2 * G_DEV, width), jnp.bfloat16),
            jax.ShapeDtypeStruct(squares.shape, jnp.float32),
            jax.ShapeDtypeStruct((2,) + squares.shape, jnp.float32),
        ),
        in_specs=[free, free, vmem, vmem, vmem],
        out_specs=(free, free, vmem, vmem),
        scratch_shapes=[
            pltpu.VMEM((heads - 1,) + squares.shape, jnp.float32),
            pltpu.VMEM(squares.shape, jnp.float32),
            pltpu.VMEM((2,) + squares.shape, jnp.float32),
            pltpu.VMEM(own_raw.shape, jnp.bfloat16),
            pltpu.SemaphoreType.DMA((6,)),
            pltpu.SemaphoreType.DMA((6,)),
            pltpu.SemaphoreType.DMA((heads - 1,)),
            pltpu.SemaphoreType.DMA((heads - 1,)),
            pltpu.SemaphoreType.DMA((copies,)),
            pltpu.SemaphoreType.DMA((copies,)),
            pltpu.SemaphoreType.DMA,
        ],
        compiler_params=pltpu.CompilerParams(collective_id=1, has_side_effects=True),
    )(key_raw, values, squares, own_raw, gain)


def collect_kernel(
    count, heads, prev_ref, next_ref, part_ref, dots_ref, weight_ref,
    from_ref, sum_ref, tot_ref, near_ref, extra_ref,
    slots, half, yslots, quarter, zslot, hslots, total_buf, near_buf, extra_buf, eslots,
    wsend, wrecv, gsend, grecv, hsend, hrecv, esend, erecv,
):
    y, z, low, yn, other_z, y_peers, low_peers, after, before = places(count)
    peers = head_peers(heads)
    greet(peers + [after, before, other_z] + y_peers + low_peers)
    wsems, hsems, gsems, esems = (wsend, wrecv), (hsend, hrecv), (gsend, grecv), (esend, erecv)
    dotted = start_all(dots_ref, hslots, hsems, peers)
    sent = []
    for o, peer in enumerate(low_peers):
        copy = remote(part_ref.at[lax.rem(low + 1 + o, LOW)], slots.at[o], gsems, o, peer)
        copy.start()
        sent.append(copy)
    moved = [
        remote(next_ref, from_ref.at[0], wsems, 0, after),
        remote(prev_ref, from_ref.at[1], wsems, 1, before),
    ]
    for copy in moved:
        copy.start()
    total = add_arrivals(dots_ref[...], hslots, dotted)
    total_buf[...] = total
    tot_ref[...] = total
    near = [
        remote(total_buf, near_buf.at[0], wsems, 2, after),
        remote(total_buf, near_buf.at[1], wsems, 3, before),
    ]
    for copy in near:
        copy.start()
    half[...] = add_arrivals(part_ref[low], slots, sent)
    ysent = []
    for o, peer in enumerate(y_peers):
        copy = remote(half.at[lax.rem(y + 1 + o, yn)], yslots.at[o], gsems, LOW - 1 + o, peer)
        copy.start()
        ysent.append(copy)
    row = add_arrivals(half[y], yslots, ysent)
    quarter[...] = row
    swap = remote(quarter, zslot, gsems, LOW - 1 + yn - 1, other_z)
    swap.start()
    swap.wait_recv()
    reduced = row + zslot[...]
    sum_ref[...] = reduced
    share = jnp.sum(reduced * weight_ref[...], axis=1, keepdims=True)
    extra = jnp.broadcast_to(share, extra_buf.shape)
    extra_buf[...] = extra
    extras = start_all(extra_buf, eslots, esems, peers)
    extra_ref[...] = add_arrivals(extra, eslots, extras)
    for copy in near:
        copy.wait()
    near_ref[...] = near_buf[...]
    for copy in moved:
        copy.wait()
    for copy in sent + ysent + [swap] + dotted + extras:
        copy.wait_send()


def collect(to_prev, to_next, parts, dots, weight):
    count = lax.axis_size("ctx")
    heads = lax.axis_size("head")
    yn = count // (LOW * ZN)
    rows, width = parts.shape[2:]
    copies = LOW - 1 + yn
    vmem = pl.BlockSpec(memory_space=pltpu.VMEM)
    free = pl.BlockSpec(memory_space=pl.ANY)
    return pl.pallas_call(
        functools.partial(collect_kernel, count, heads),
        out_shape=(
            jax.ShapeDtypeStruct((2,) + to_prev.shape, jnp.bfloat16),
            jax.ShapeDtypeStruct((rows, width), jnp.float32),
            jax.ShapeDtypeStruct(dots.shape, jnp.float32),
            jax.ShapeDtypeStruct((2,) + dots.shape, jnp.float32),
            jax.ShapeDtypeStruct((rows, 128), jnp.float32),
        ),
        in_specs=[free, free, vmem, vmem, vmem],
        out_specs=(free, vmem, vmem, vmem, vmem),
        scratch_shapes=[
            pltpu.VMEM((LOW - 1, yn, rows, width), jnp.float32),
            pltpu.VMEM((yn, rows, width), jnp.float32),
            pltpu.VMEM((yn - 1, rows, width), jnp.float32),
            pltpu.VMEM((rows, width), jnp.float32),
            pltpu.VMEM((rows, width), jnp.float32),
            pltpu.VMEM((heads - 1,) + dots.shape, jnp.float32),
            pltpu.VMEM(dots.shape, jnp.float32),
            pltpu.VMEM((2,) + dots.shape, jnp.float32),
            pltpu.VMEM((rows, 128), jnp.float32),
            pltpu.VMEM((heads - 1, rows, 128), jnp.float32),
            pltpu.SemaphoreType.DMA((4,)),
            pltpu.SemaphoreType.DMA((4,)),
            pltpu.SemaphoreType.DMA((copies,)),
            pltpu.SemaphoreType.DMA((copies,)),
            pltpu.SemaphoreType.DMA((heads - 1,)),
            pltpu.SemaphoreType.DMA((heads - 1,)),
            pltpu.SemaphoreType.DMA((heads - 1,)),
            pltpu.SemaphoreType.DMA((heads - 1,)),
        ],
        compiler_params=pltpu.CompilerParams(collective_id=2, has_side_effects=True),
    )(to_prev, to_next, parts, dots, weight)


def dot(a, b, dims):
    return lax.dot_general(a, b, (dims, ((), ())), preferred_element_type=jnp.float32)


ROWS = ((1,), (0,))
TURNED = ((1,), (1,))
DOWN = ((0,), (0,))


def attention_kernel(
    start_ref, live_ref, tot_ref, near_ref, qgain_ref, kgain_ref,
    q_ref, g_ref, key_ref, val_ref, win_ref, glob_ref,
    dq_ref, prev_ref, next_ref, own_ref, dglob_ref, dots_ref,
    inverses, queries, keys, vals, dkeys, dvals, dot_sums,
):
    tokens = q_ref.shape[0]
    span = KEYS * TILE
    factor = HEAD_DIM ** (-0.5)

    @pl.when(pl.program_id(0) == 0)
    def _():
        own = lax.rsqrt(tot_ref[...] / D + EPSILON)
        near = lax.rsqrt(near_ref[...] / D + EPSILON)
        lines = [own[0:1], own[1:2], near[0, 2:3], near[0, 3:4]]
        lines += [own[2:3], own[3:4], near[1, 2:3], near[1, 3:4]]
        for index, line in enumerate(lines):
            inverses[index * TILE : (index + 1) * TILE] = jnp.broadcast_to(line, (TILE, TILE)).T
        dot_sums[...] = jnp.zeros_like(dot_sums)

    qgain = qgain_ref[...]
    kgain = kgain_ref[...]
    query_rows = q_ref[...].astype(jnp.float32)
    queries[...] = (query_rows * inverses[0:tokens] * qgain).astype(jnp.bfloat16)
    blocks = [win_ref[0, 0], key_ref[...], win_ref[1, 0]]
    for index, block in enumerate(blocks):
        rows = slice(index * tokens, (index + 1) * tokens)
        scale = inverses[(index + 1) * tokens : (index + 2) * tokens]
        keys[rows] = (block.astype(jnp.float32) * scale * kgain).astype(jnp.bfloat16)
    vals[0:tokens] = win_ref[0, 1]
    vals[tokens : 2 * tokens] = val_ref[...]
    vals[2 * tokens :] = win_ref[1, 1]
    dkeys[...] = jnp.zeros_like(dkeys)
    dvals[...] = jnp.zeros_like(dvals)
    gkeys = glob_ref[0]
    gvals = glob_ref[1]
    live = live_ref[...] > 0
    gdk = 0.0
    gdv = 0.0
    for tile in range(tokens // TILE):
        rows = slice(tile * TILE, (tile + 1) * TILE)
        window = pl.ds(pl.multiple_of(start_ref[tile] * TILE, TILE), span)
        query = queries[rows]
        grad = g_ref[rows]
        wkeys = keys[window]
        wvals = vals[window]
        score_w = dot(query, wkeys, TURNED) * factor
        score_g = jnp.where(live, dot(query, gkeys, TURNED) * factor, -jnp.inf)
        largest = jnp.maximum(
            jnp.max(score_w, axis=1, keepdims=True), jnp.max(score_g, axis=1, keepdims=True)
        )
        exp_w = jnp.exp(score_w - largest)
        exp_g = jnp.exp(score_g - largest)
        inverse = 1.0 / (
            jnp.sum(exp_w, axis=1, keepdims=True) + jnp.sum(exp_g, axis=1, keepdims=True)
        )
        prob_w = exp_w * inverse
        prob_g = exp_g * inverse
        low_w = prob_w.astype(jnp.bfloat16)
        low_g = prob_g.astype(jnp.bfloat16)
        attended = (dot(low_w, wvals, ROWS) + dot(low_g, gvals, ROWS)).astype(jnp.bfloat16)
        delta = jnp.sum(
            grad.astype(jnp.float32) * attended.astype(jnp.float32), axis=1, keepdims=True
        )
        ds_w = (prob_w * (dot(grad, wvals, TURNED) - delta) * factor).astype(jnp.bfloat16)
        ds_g = (prob_g * (dot(grad, gvals, TURNED) - delta) * factor).astype(jnp.bfloat16)
        dq_ref[rows] = dot(ds_w, wkeys, ROWS) + dot(ds_g, gkeys, ROWS)
        dkeys[window] += dot(ds_w, query, DOWN)
        dvals[window] += dot(low_w, grad, DOWN)
        gdk = gdk + dot(ds_g, query, DOWN)
        gdv = gdv + dot(low_g, grad, DOWN)
    for pair_index, cat in enumerate((dkeys, dvals)):
        prev_ref[pair_index] = cat[0:tokens].astype(jnp.bfloat16)
        own_ref[pair_index] = cat[tokens : 2 * tokens]
        next_ref[pair_index] = cat[2 * tokens :].astype(jnp.bfloat16)
    dglob_ref[0] = gdk
    dglob_ref[1] = gdv
    dot_sums[0:tokens] += dq_ref[...] * qgain * query_rows
    for index, block in enumerate(blocks):
        rows = slice(index * tokens, (index + 1) * tokens)
        dot_sums[(index + 1) * tokens : (index + 2) * tokens] += (
            dkeys[rows] * kgain * block.astype(jnp.float32)
        )

    @pl.when(pl.program_id(0) == pl.num_programs(0) - 1)
    def _():
        for index in range(dots_ref.shape[0]):
            turned = dot_sums[index * TILE : (index + 1) * TILE].T
            dots_ref[index : index + 1] = jnp.sum(turned, axis=0, keepdims=True)


def attention(starts, live, totals, near, qgain, kgain, query, out_grad, key, val, window, globs):
    tokens, width = query.shape
    count = globs.shape[1]
    whole = pl.BlockSpec(memory_space=pltpu.VMEM)
    flat = pl.BlockSpec((tokens, HEAD_DIM), lambda h: (0, h))
    gain = pl.BlockSpec((1, HEAD_DIM), lambda h: (0, h))
    pair = pl.BlockSpec((2, tokens, HEAD_DIM), lambda h: (0, 0, h))
    glob = pl.BlockSpec((2, count, HEAD_DIM), lambda h: (0, 0, h))
    pair_shape = (2, tokens, width)
    lines = 4 * tokens // TILE
    return pl.pallas_call(
        attention_kernel,
        grid=(width // HEAD_DIM,),
        out_shape=(
            jax.ShapeDtypeStruct((tokens, width), jnp.float32),
            jax.ShapeDtypeStruct(pair_shape, jnp.bfloat16),
            jax.ShapeDtypeStruct(pair_shape, jnp.bfloat16),
            jax.ShapeDtypeStruct(pair_shape, jnp.float32),
            jax.ShapeDtypeStruct((2, count, width), jnp.float32),
            jax.ShapeDtypeStruct((lines, TILE), jnp.float32),
        ),
        in_specs=[
            pl.BlockSpec(memory_space=pltpu.SMEM),
            whole,
            whole,
            whole,
            gain,
            gain,
            flat,
            flat,
            flat,
            flat,
            pl.BlockSpec((2, 2, tokens, HEAD_DIM), lambda h: (0, 0, 0, h)),
            glob,
        ],
        out_specs=(flat, pair, pair, pair, glob, pl.BlockSpec((lines, TILE), lambda h: (0, 0))),
        scratch_shapes=[
            pltpu.VMEM((4 * tokens, HEAD_DIM), jnp.float32),
            pltpu.VMEM((tokens, HEAD_DIM), jnp.bfloat16),
            pltpu.VMEM((3 * tokens, HEAD_DIM), jnp.bfloat16),
            pltpu.VMEM((3 * tokens, HEAD_DIM), jnp.bfloat16),
            pltpu.VMEM((3 * tokens, HEAD_DIM), jnp.float32),
            pltpu.VMEM((3 * tokens, HEAD_DIM), jnp.float32),
            pltpu.VMEM((4 * tokens, HEAD_DIM), jnp.float32),
        ],
    )(starts, live, totals, near, qgain, kgain, query, out_grad, key, val, window, globs)


def body(
    query_raw, key_raw, values, out_grad, query_gain, key_gain, key_tiles, global_ids, readers
):
    tokens_here, width = query_raw.shape
    tiles_here = tokens_here // TILE
    count = lax.axis_size("ctx")
    yn = count // (LOW * ZN)
    device = lax.axis_index("ctx")
    query_rows = query_raw.astype(jnp.float32)
    key_rows = key_raw.astype(jnp.float32)
    own_rows = global_ids - device * tokens_here
    own_keys = key_raw[own_rows].astype(jnp.float32)
    own_vals = values[own_rows].astype(jnp.float32)
    own_squares = jnp.sum(own_keys * own_keys, axis=1)
    squares = jnp.concatenate(
        [
            jnp.sum(query_rows * query_rows, axis=1).reshape(tiles_here, TILE),
            jnp.sum(key_rows * key_rows, axis=1).reshape(tiles_here, TILE),
            jnp.broadcast_to(own_squares[:, None], (G_DEV, TILE)),
            jnp.zeros((G_DEV, TILE), jnp.float32),
        ]
    )
    qgain = query_gain[None, :]
    kgain = key_gain[None, :]
    window, globs, totals, near = spread(
        key_raw, values, squares, jnp.concatenate([own_keys, own_vals]), kgain
    )
    globs = (
        globs.reshape(LOW, yn, ZN, 2, G_DEV, width)
        .transpose(3, 1, 2, 0, 4, 5)
        .reshape(2, count * G_DEV, width)
    )
    live = jnp.repeat(readers, G_DEV, axis=1)
    starts = jnp.clip(key_tiles[:, 0] - (device - 1) * tiles_here, 0, 3 * tiles_here - KEYS)
    grad_query, to_prev, to_next, own_grads, glob_grads, dots = attention(
        starts, live, totals, near, qgain, kgain, query_raw, out_grad, key_raw, values, window, globs
    )
    parts = (
        glob_grads.reshape(2, yn, ZN, LOW, G_DEV, width)
        .transpose(3, 1, 2, 0, 4, 5)
        .reshape(LOW, yn, ZN * 2 * G_DEV, width)
    )
    z = lax.rem(device // LOW, ZN)
    weight = jnp.where(
        (jnp.arange(ZN)[:, None] == z)[:, :, None, None] & (jnp.arange(2) == 0)[None, :, None, None],
        (own_keys * key_gain)[None, None],
        0.0,
    ).reshape(ZN * 2 * G_DEV, width)
    arrived, reduced, dot_totals, dot_near, extra = collect(to_prev, to_next, parts, dots, weight)
    mine = lax.dynamic_index_in_dim(
        reduced.reshape(ZN, 2, G_DEV, width), z, 0, keepdims=False
    )
    extra = extra.reshape(ZN, 2, G_DEV, 128)[:, 0, :, 0].sum(axis=0)
    home = own_grads + arrived[0].astype(jnp.float32) + arrived[1].astype(jnp.float32)
    spots = jnp.arange(tokens_here, dtype=jnp.int32)
    query_dot = dot_totals[0:2].reshape(-1)
    key_dot = (dot_totals[4:6] + dot_near[0, 6:8] + dot_near[1, 2:4]).reshape(-1)
    for index in range(G_DEV):
        here = spots == own_rows[index]
        home = home + jnp.where(here[:, None], mine[:, index][:, None, :], 0.0)
        key_dot = key_dot + jnp.where(here, extra[index], 0.0)
    query_inv = lax.rsqrt(totals[0:2].reshape(-1, 1) / D + EPSILON)
    key_inv = lax.rsqrt(totals[2:4].reshape(-1, 1) / D + EPSILON)
    query_grad = norm_grad(query_rows, query_inv, grad_query * query_gain, query_dot)
    key_grad = norm_grad(key_rows, key_inv, home[0] * key_gain, key_dot)
    return (query_grad, key_grad, home[1].astype(jnp.bfloat16))


def solution(mesh):
    return jax.shard_map(
        body,
        mesh=mesh,
        in_specs=(
            P("ctx", "head"),
            P("ctx", "head"),
            P("ctx", "head"),
            P("ctx", "head"),
            P("head"),
            P("head"),
            P("ctx", None),
            P("ctx"),
            P("ctx", None),
        ),
        out_specs=(P("ctx", "head"), P("ctx", "head"), P("ctx", "head")),
        check_vma=False,
    )
```

time: 156 us -> 164 us (1.051)
  the two profiles are of different devices: /device:TPU:32 before, /device:TPU:7 now
where the time goes in v2:
time: 164 us
  Pallas kernels  133 us (81%)
  other arithmetic  16 us (10%)
  local copies, waits for them, and re-layouts  14.2 us (9%)
    pallas_call x1, Pallas kernels, spread(): pl.pallas_call(functools.partial(spread_kernel, count, heads), out_shape=...  65.2 us
    pallas_call x1, Pallas kernels, collect(): pl.pallas_call(functools.partial(collect_kernel, count, heads), out_shape...  55 us
    pallas_call x1, Pallas kernels, attention(): pl.pallas_call(attention_kernel, grid=(width // HEAD_DIM,), out_shape=(ja...  12.3 us
    div x2, other arithmetic, norm_grad(): coeffs[:, None] / D  4.04 us

profile of v2, /device:TPU:7, one launch (start us, length us, event | category | flops | bytes accessed | tf_op | source)
XLA Modules:
  0.0 163.7 jit_solution(7009540580518367140)
XLA Ops:
  0.6 0.0 copy-start.7
  0.6 1.4 clamp_reduce_fusion.start_ref
  2.0 0.7 broadcast_in_dim.111
  2.8 0.7 broadcast_in_dim.112.live_ref
  3.5 1.1 fusion.6
  4.6 1.1 fusion.2
  5.7 0.1 pad.5.clone
  5.8 0.7 compare_select_fusion
  6.5 1.6 gather_fusion
  8.0 0.8 broadcast_multiply_fusion
  8.9 0.1 pad.4.clone
  8.9 0.7 maximum_maximum_fusion.sq_ref
  9.6 1.6 gather_fusion.1
  11.2 0.6 pad_maximum_fusion.raw_ref
  11.8 1.3 broadcast_in_dim.110.gain_ref.kgain_ref
  13.1 65.2 %shard_map.115 = (bf16[2,2,256,640]{3,2,1,0:T(8,128)(2,1)}, bf16[8,4,2,4,640]{4,3,2,1,0:T(4,128)(2,1)}, f32[8,128]{1,0:T(8,128)}, f32[2,8,128]{2,1,0:T(8,128)}) custom-call(bf16[256,640]{1,0:T(8,128)(2,1)} %key_ref.3, bf16[256,640]{1,0:T(8,128)(2,1)} %val_ref.3, f32[8,128]{1,0:T(8,128)} %maximum_maximum_fusion.sq_ref, f32[4,640]{1,0:T(4,128)} %pad_maximum_fusion.raw_ref, ...), custom_call_target="tpu_custom_call" | custom-call | tf_op jit(solution)/shard_map/pallas_call | solution.py:155
  78.3 0.0 copy-done.7
  78.3 0.6 broadcast_in_dim.113.qgain_ref
  78.9 1.1 reshape.189
  80.0 0.2 copy.23
  80.2 0.8 reshape.190.glob_ref
  81.1 12.3 %shard_map.116 = (f32[256,640]{1,0:T(8,128)}, bf16[2,256,640]{2,1,0:T(8,128)(2,1)}, bf16[2,256,640]{2,1,0:T(8,128)(2,1)}, f32[2,256,640]{2,1,0:T(8,128)}, f32[2,128,640]{2,1,0:T(8,128)}, /*index=5*/f32[8,128]{1,0:T(8,128)}) custom-call(s32[2]{0:T(128)} %clamp_reduce_fusion.start_ref, s32[1,128]{1,0:T(1,128)} %broadcast_in_dim.112.live_ref, ...), custom_call_target="tpu_custom_call" | custom-call | tf_op jit(solution)/shard_map/pallas_call | solution.py:393
  93.4 1.5 reshape.191
  94.9 0.1 copy.22
  95.0 1.3 reshape.192.part_ref
  96.3 0.0 copy-start.6
  96.3 0.0 copy-start.1
  96.4 0.1 broadcast_and_fusion
  96.4 0.1 broadcast_in_dim.114
  96.5 0.1 broadcast_in_dim.115
  96.6 0.7 broadcast_select_fusion.weight_ref
  97.3 0.0 copy-start.2
  97.3 55.0 %shard_map.117 = (bf16[2,2,256,640]{3,2,1,0:T(8,128)(2,1)}, f32[8,640]{1,0:T(8,128)}, f32[8,128]{1,0:T(8,128)}, f32[2,8,128]{2,1,0:T(8,128)}, f32[8,128]{1,0:T(8,128)}) custom-call(bf16[2,256,640]{2,1,0:T(8,128)(2,1)} %get-tuple-element.23.prev_ref, bf16[2,256,640]{2,1,0:T(8,128)(2,1)} %get-tuple-element.24.next_ref, f32[8,4,8,640]{3,2,1,0:T(8,128)} %reshape.192.part_ref, ...), custom_call_target="tpu_custom_call" | custom-call | tf_op jit(solution)/shard_map/pallas_call | solution.py:248
  152.3 0.0 copy-start.5
  152.3 0.0 copy-start.3
  152.4 0.8 multiply_bitcast_fusion
  153.1 0.0 copy-done.6
  153.2 0.0 copy-done.1
  153.2 2.0 %fusion.5 = bf16[256,640]{1,0:T(8,128)(2,1)} fusion(bf16[256,640]{1,0:T(8,128)(2,1)S(1)} %copy-done.1, f32[256,640]{1,0:T(8,128)} %get-tuple-element.22, f32[256]{0:T(256)S(1)} %multiply_bitcast_fusion, f32[256]{0:T(256)S(1)} %get-tuple-element.40, f32[640]{0:T(1024)S(1)} %copy-done.7, f32[256]{0:T(256)S(1)} %get-tuple-element.38), kind=kLoop, calls=%fused_computation.13 | loop fusion | flops 1146880 | bytes 1316352 | tf_op jit(solution)/shard_map/convert_element_type | solution.py:24
  155.2 0.0 copy-done.5
  155.3 0.6 fusion.17
  155.9 1.3 iota_compare_fusion
  157.2 0.0 copy-done.2
  157.2 0.0 copy-done.3
  157.2 0.0 copy-start.8
  157.2 0.0 copy-start
  157.2 0.0 copy-start.4
  157.2 0.4 fusion.1
  157.6 0.3 copy-done.8
  157.9 0.1 slice_reduce_fusion
  158.0 0.7 fusion.16
  158.7 3.3 %fusion.14 = f32[256]{0:T(256)S(1)} fusion(f32[2,8,128]{2,1,0:T(8,128)} %get-tuple-element.31, f32[8,128]{1,0:T(8,128)} %get-tuple-element.27, f32[]{:T(128)} %bitcast.19, f32[]{:T(128)} %bitcast.18, s32[]{:T(128)} %bitcast.10, s32[]{:T(128)} %bitcast.12), kind=kLoop, calls=%fused_computation.40 | loop fusion | flops 2304 | bytes 4112 | tf_op jit(solution)/shard_map/div | solution.py:24
  161.9 0.0 copy-done
  161.9 0.0 copy-done.4
  161.9 0.9 fusion.9
  162.9 0.8 fusion.12
  (14 shorter events, 0.1 us)
Async XLA Ops:
  0.6 77.7 %copy-start.7 = (f32[640]{0:T(1024)S(1)}, f32[640]{0:T(1024)}, u32[]{:S(2)}) copy-start(f32[640]{0:T(1024)} %param.13) | copy-start | bytes 7684
  96.3 56.9 %copy-start.6 = (f32[8,128]{1,0:T(8,128)S(1)}, f32[8,128]{1,0:T(8,128)}, u32[]{:S(2)}) copy-start(f32[8,128]{1,0:T(8,128)} %get-tuple-element.18.tot_ref) | copy-start | bytes 12292
  96.3 56.9 %copy-start.1 = (bf16[256,640]{1,0:T(8,128)(2,1)S(1)}, bf16[256,640]{1,0:T(8,128)(2,1)}, u32[]{:S(2)}) copy-start(bf16[256,640]{1,0:T(8,128)(2,1)} %q_ref.1) | copy-start | bytes 983044
  97.3 59.9 %copy-start.2 = (f32[2,256,640]{2,1,0:T(8,128)S(1)}, f32[2,256,640]{2,1,0:T(8,128)}, u32[]{:S(2)}) copy-start(f32[2,256,640]{2,1,0:T(8,128)} %get-tuple-element.28) | copy-start | bytes 3932164
  152.3 2.9 %copy-start.5 = (f32[8,640]{1,0:T(8,128)S(1)}, f32[8,640]{1,0:T(8,128)}, u32[]{:S(2)}) copy-start(f32[8,640]{1,0:T(8,128)} %get-tuple-element.30) | copy-start | bytes 61444
  152.3 4.9 %copy-start.3 = (bf16[2,2,256,640]{3,2,1,0:T(8,128)(2,1)S(1)}, bf16[2,2,256,640]{3,2,1,0:T(8,128)(2,1)}, u32[]{:S(2)}) copy-start(bf16[2,2,256,640]{3,2,1,0:T(8,128)(2,1)} %get-tuple-element.29) | copy-start | bytes 3932164
  157.2 0.7 copy-start.8
  157.2 4.7 %copy-start = (bf16[256,640]{1,0:T(8,128)(2,1)S(1)}, bf16[256,640]{1,0:T(8,128)(2,1)}, u32[]{:S(2)}) copy-start(bf16[256,640]{1,0:T(8,128)(2,1)} %key_ref.3) | copy-start | bytes 983044
  157.2 4.7 %copy-start.4 = (f32[640]{0:T(1024)S(1)}, f32[640]{0:T(1024)}, u32[]{:S(2)}) copy-start(f32[640]{0:T(1024)} %param.14) | copy-start | bytes 7684

commit v3 on v2

--- a/solution.py
+++ b/solution.py
@@ -20,8 +20,13 @@
 EPSILON = 1e-06
 
 
-def norm_grad(as_float, inverse, scaled, coeffs):
-    return (inverse * scaled - as_float * inverse**3 * (coeffs[:, None] / D)).astype(jnp.bfloat16)
+def dot(a, b, dims):
+    return lax.dot_general(a, b, (dims, ((), ())), preferred_element_type=jnp.float32)
+
+
+ROWS = ((1,), (0,))
+TURNED = ((1,), (1,))
+DOWN = ((0,), (0,))
 
 
 def greet(targets):
@@ -79,29 +84,60 @@
     return y, z, low, yn, other_z, y_peers, low_peers, after, before
 
 
+def own_tokens(ids_ref, first, key_ref, val_ref):
+    tokens = key_ref.shape[0]
+    rows = lax.broadcasted_iota(jnp.int32, (8, tokens), 0)
+    spots = lax.broadcasted_iota(jnp.int32, (8, tokens), 1)
+    picks = jnp.zeros((8, tokens), jnp.float32)
+    for index in range(G_DEV):
+        hit = (rows % G_DEV == index) & (spots == ids_ref[index] - first)
+        picks = jnp.where(hit, 1.0, picks)
+    picks = picks.astype(jnp.bfloat16)
+    keys = dot(picks, key_ref[...], ROWS)[0:4]
+    vals = dot(picks, val_ref[...], ROWS)[0:4]
+    is_key = lax.broadcasted_iota(jnp.int32, keys.shape, 0) < G_DEV
+    return jnp.where(is_key, keys, vals)
+
+
 def spread_kernel(
-    count, heads, key_ref, val_ref, sq_ref, raw_ref, gain_ref,
+    count, heads, ids_ref, query_ref, key_ref, val_ref, gain_ref,
     win_ref, glob_ref, tot_ref, near_ref,
-    hslots, total_buf, near_buf, own_buf, wsend, wrecv, hsend, hrecv, gsend, grecv, lsem,
+    sq_buf, hslots, total_buf, near_buf, own_buf, wsend, wrecv, hsend, hrecv, gsend, grecv, lsem,
 ):
     y, z, low, yn, other_z, y_peers, low_peers, after, before = places(count)
     peers = head_peers(heads)
     greet(peers + [after, before, other_z] + y_peers + low_peers)
     wsems, hsems, gsems = (wsend, wrecv), (hsend, hrecv), (gsend, grecv)
-    summed = start_all(sq_ref, hslots, hsems, peers)
     moved = [
         remote(key_ref, win_ref.at[0, 0], wsems, 0, after),
         remote(key_ref, win_ref.at[1, 0], wsems, 1, before),
+        remote(val_ref, win_ref.at[0, 1], wsems, 2, after),
+        remote(val_ref, win_ref.at[1, 1], wsems, 3, before),
     ]
     for copy in moved:
         copy.start()
-    total = add_arrivals(sq_ref[...], hslots, summed)
+    tokens, width = key_ref.shape
+    first = lax.axis_index("ctx") * tokens
+    line = 0
+    for ref in (query_ref, key_ref):
+        for start in range(0, tokens, TILE):
+            folded = jnp.zeros((TILE, TILE), jnp.float32)
+            for column in range(0, width, TILE):
+                block = ref[start : start + TILE, column : column + TILE].astype(jnp.float32)
+                folded = folded + block * block
+            sq_buf[line : line + 1] = jnp.sum(folded.T, axis=0, keepdims=True)
+            line += 1
+    raw = own_tokens(ids_ref, first, key_ref, val_ref)
+    own_squares = jnp.sum(raw * raw, axis=1, keepdims=True)
+    sq_buf[4:8] = jnp.broadcast_to(own_squares, (4, TILE))
+    squares = sq_buf[...]
+    summed = start_all(sq_buf, hslots, hsems, peers)
+    total = add_arrivals(squares, hslots, summed)
     total_buf[...] = total
     tot_ref[...] = total
-    raw = raw_ref[...]
     inverse = lax.rsqrt(total[4:8, 0:1] / D + EPSILON)
     is_key = lax.broadcasted_iota(jnp.int32, raw.shape, 0) < G_DEV
-    own_buf[...] = jnp.where(is_key, raw * inverse * gain_ref[...], raw).astype(jnp.bfloat16)
+    own_buf[...] = jnp.where(is_key, raw * inverse * gain_ref[1:2], raw).astype(jnp.bfloat16)
     swap = remote(own_buf, glob_ref.at[low, y, z], gsems, 0, other_z)
     swap.start()
     local = pltpu.make_async_copy(own_buf, glob_ref.at[low, y, z], lsem)
@@ -126,29 +162,24 @@
         copy = remote(glob_ref.at[low], glob_ref.at[low], gsems, yn + o, peer)
         copy.start()
         sent.append(copy)
-    late = [
-        remote(val_ref, win_ref.at[0, 1], wsems, 2, after),
-        remote(val_ref, win_ref.at[1, 1], wsems, 3, before),
-    ]
-    for copy in late:
-        copy.start()
     for o, peer in enumerate(low_peers):
         source = lax.rem(low + LOW - 1 - o, LOW)
         remote(glob_ref.at[source], glob_ref.at[source], gsems, yn + o, peer).wait_recv()
     for copy in near:
         copy.wait()
     near_ref[...] = near_buf[...]
-    for copy in moved + late:
+    for copy in moved:
         copy.wait()
     for copy in sent + summed:
         copy.wait_send()
 
 
-def spread(key_raw, values, squares, own_raw, gain):
+def spread(ids, query_raw, key_raw, values, gains):
     count = lax.axis_size("ctx")
     heads = lax.axis_size("head")
     yn = count // (LOW * ZN)
-    width = own_raw.shape[-1]
+    width = key_raw.shape[-1]
+    lines = (8, TILE)
     copies = yn + LOW - 1
     vmem = pl.BlockSpec(memory_space=pltpu.VMEM)
     free = pl.BlockSpec(memory_space=pl.ANY)
@@ -157,16 +188,17 @@
         out_shape=(
             jax.ShapeDtypeStruct((2, 2) + key_raw.shape, jnp.bfloat16),
             jax.ShapeDtypeStruct((LOW, yn, ZN, 2 * G_DEV, width), jnp.bfloat16),
-            jax.ShapeDtypeStruct(squares.shape, jnp.float32),
-            jax.ShapeDtypeStruct((2,) + squares.shape, jnp.float32),
+            jax.ShapeDtypeStruct(lines, jnp.float32),
+            jax.ShapeDtypeStruct((2,) + lines, jnp.float32),
         ),
-        in_specs=[free, free, vmem, vmem, vmem],
+        in_specs=[pl.BlockSpec(memory_space=pltpu.SMEM), vmem, vmem, vmem, vmem],
         out_specs=(free, free, vmem, vmem),
         scratch_shapes=[
-            pltpu.VMEM((heads - 1,) + squares.shape, jnp.float32),
-            pltpu.VMEM(squares.shape, jnp.float32),
-            pltpu.VMEM((2,) + squares.shape, jnp.float32),
-            pltpu.VMEM(own_raw.shape, jnp.bfloat16),
+            pltpu.VMEM(lines, jnp.float32),
+            pltpu.VMEM((heads - 1,) + lines, jnp.float32),
+            pltpu.VMEM(lines, jnp.float32),
+            pltpu.VMEM((2,) + lines, jnp.float32),
+            pltpu.VMEM((2 * G_DEV, width), jnp.bfloat16),
             pltpu.SemaphoreType.DMA((6,)),
             pltpu.SemaphoreType.DMA((6,)),
             pltpu.SemaphoreType.DMA((heads - 1,)),
@@ -176,11 +208,11 @@
             pltpu.SemaphoreType.DMA,
         ],
         compiler_params=pltpu.CompilerParams(collective_id=1, has_side_effects=True),
-    )(key_raw, values, squares, own_raw, gain)
+    )(ids, query_raw, key_raw, values, gains)
 
 
 def collect_kernel(
-    count, heads, prev_ref, next_ref, part_ref, dots_ref, weight_ref,
+    count, heads, ids_ref, prev_ref, next_ref, part_ref, dots_ref, key_ref, gain_ref,
     from_ref, sum_ref, tot_ref, near_ref, extra_ref,
     slots, half, yslots, quarter, zslot, hslots, total_buf, near_buf, extra_buf, eslots,
     wsend, wrecv, gsend, grecv, hsend, hrecv, esend, erecv,
@@ -192,7 +224,7 @@
     dotted = start_all(dots_ref, hslots, hsems, peers)
     sent = []
     for o, peer in enumerate(low_peers):
-        copy = remote(part_ref.at[lax.rem(low + 1 + o, LOW)], slots.at[o], gsems, o, peer)
+        copy = remote(part_ref.at[:, lax.rem(low + 1 + o, LOW)], slots.at[o], gsems, o, peer)
         copy.start()
         sent.append(copy)
     moved = [
@@ -210,7 +242,13 @@
     ]
     for copy in near:
         copy.start()
-    half[...] = add_arrivals(part_ref[low], slots, sent)
+    tokens = key_ref.shape[0]
+    raw = own_tokens(ids_ref, lax.axis_index("ctx") * tokens, key_ref, key_ref) * gain_ref[1:2]
+    summed = add_arrivals(part_ref[:, low], slots, sent)
+    each = ZN * G_DEV
+    for row in range(yn):
+        half[row, 0:each] = summed[0, row * each : (row + 1) * each]
+        half[row, each : 2 * each] = summed[1, row * each : (row + 1) * each]
     ysent = []
     for o, peer in enumerate(y_peers):
         copy = remote(half.at[lax.rem(y + 1 + o, yn)], yslots.at[o], gsems, LOW - 1 + o, peer)
@@ -223,8 +261,8 @@
     swap.wait_recv()
     reduced = row + zslot[...]
     sum_ref[...] = reduced
-    share = jnp.sum(reduced * weight_ref[...], axis=1, keepdims=True)
-    extra = jnp.broadcast_to(share, extra_buf.shape)
+    share = jnp.sum(reduced[0:each] * raw, axis=1, keepdims=True)
+    extra = jnp.broadcast_to(jnp.concatenate([share, share]), extra_buf.shape)
     extra_buf[...] = extra
     extras = start_all(extra_buf, eslots, esems, peers)
     extra_ref[...] = add_arrivals(extra, eslots, extras)
@@ -237,11 +275,12 @@
         copy.wait_send()
 
 
-def collect(to_prev, to_next, parts, dots, weight):
+def collect(ids, to_prev, to_next, parts, dots, key_raw, gains):
     count = lax.axis_size("ctx")
     heads = lax.axis_size("head")
     yn = count // (LOW * ZN)
-    rows, width = parts.shape[2:]
+    width = parts.shape[-1]
+    rows = 2 * ZN * G_DEV
     copies = LOW - 1 + yn
     vmem = pl.BlockSpec(memory_space=pltpu.VMEM)
     free = pl.BlockSpec(memory_space=pl.ANY)
@@ -254,10 +293,10 @@
             jax.ShapeDtypeStruct((2,) + dots.shape, jnp.float32),
             jax.ShapeDtypeStruct((rows, 128), jnp.float32),
         ),
-        in_specs=[free, free, vmem, vmem, vmem],
+        in_specs=[pl.BlockSpec(memory_space=pltpu.SMEM), free, free, vmem, vmem, vmem, vmem],
         out_specs=(free, vmem, vmem, vmem, vmem),
         scratch_shapes=[
-            pltpu.VMEM((LOW - 1, yn, rows, width), jnp.float32),
+            pltpu.VMEM((LOW - 1, 2) + parts.shape[2:], jnp.float32),
             pltpu.VMEM((yn, rows, width), jnp.float32),
             pltpu.VMEM((yn - 1, rows, width), jnp.float32),
             pltpu.VMEM((rows, width), jnp.float32),
@@ -277,23 +316,14 @@
             pltpu.SemaphoreType.DMA((heads - 1,)),
         ],
         compiler_params=pltpu.CompilerParams(collective_id=2, has_side_effects=True),
-    )(to_prev, to_next, parts, dots, weight)
-
-
-def dot(a, b, dims):
-    return lax.dot_general(a, b, (dims, ((), ())), preferred_element_type=jnp.float32)
-
-
-ROWS = ((1,), (0,))
-TURNED = ((1,), (1,))
-DOWN = ((0,), (0,))
+    )(ids, to_prev, to_next, parts, dots, key_raw, gains)
 
 
 def attention_kernel(
-    start_ref, live_ref, tot_ref, near_ref, qgain_ref, kgain_ref,
+    tiles_ref, readers_ref, tot_ref, near_ref, gain_ref,
     q_ref, g_ref, key_ref, val_ref, win_ref, glob_ref,
     dq_ref, prev_ref, next_ref, own_ref, dglob_ref, dots_ref,
-    inverses, queries, keys, vals, dkeys, dvals, dot_sums,
+    inverses, queries, keys, vals, dkeys, dvals, dot_sums, live_buf,
 ):
     tokens = q_ref.shape[0]
     span = KEYS * TILE
@@ -308,9 +338,21 @@
         for index, line in enumerate(lines):
             inverses[index * TILE : (index + 1) * TILE] = jnp.broadcast_to(line, (TILE, TILE)).T
         dot_sums[...] = jnp.zeros_like(dot_sums)
-
-    qgain = qgain_ref[...]
-    kgain = kgain_ref[...]
+        devices = readers_ref.shape[1]
+        globals_here = glob_ref.shape[1]
+        owner = lax.broadcasted_iota(jnp.int32, (devices, globals_here), 0)
+        place = lax.broadcasted_iota(jnp.int32, (devices, globals_here), 1) // G_DEV
+        groups = devices // LOW
+        match = (owner % LOW == place // groups) & (owner // LOW == place % groups)
+        flags = jnp.broadcast_to((readers_ref[...] > 0).astype(jnp.float32), (8, devices))
+        live_buf[...] = dot(
+            flags.astype(jnp.bfloat16), match.astype(jnp.float32).astype(jnp.bfloat16), ROWS
+        )
+
+    qgain = gain_ref[0:1]
+    kgain = gain_ref[1:2]
+    first_tile = (lax.axis_index("ctx") - 1) * (tokens // TILE)
+    last_start = 3 * (tokens // TILE) - KEYS
     query_rows = q_ref[...].astype(jnp.float32)
     queries[...] = (query_rows * inverses[0:tokens] * qgain).astype(jnp.bfloat16)
     blocks = [win_ref[0, 0], key_ref[...], win_ref[1, 0]]
@@ -325,12 +367,13 @@
     dvals[...] = jnp.zeros_like(dvals)
     gkeys = glob_ref[0]
     gvals = glob_ref[1]
-    live = live_ref[...] > 0
+    live = live_buf[0:1] > 0
     gdk = 0.0
     gdv = 0.0
     for tile in range(tokens // TILE):
         rows = slice(tile * TILE, (tile + 1) * TILE)
-        window = pl.ds(pl.multiple_of(start_ref[tile] * TILE, TILE), span)
+        start = jnp.clip(tiles_ref[tile, 0] - first_tile, 0, last_start)
+        window = pl.ds(pl.multiple_of(start * TILE, TILE), span)
         query = queries[rows]
         grad = g_ref[rows]
         wkeys = keys[window]
@@ -380,12 +423,12 @@
             dots_ref[index : index + 1] = jnp.sum(turned, axis=0, keepdims=True)
 
 
-def attention(starts, live, totals, near, qgain, kgain, query, out_grad, key, val, window, globs):
+def attention(tiles, readers, totals, near, gains, query, out_grad, key, val, window, globs):
     tokens, width = query.shape
     count = globs.shape[1]
     whole = pl.BlockSpec(memory_space=pltpu.VMEM)
     flat = pl.BlockSpec((tokens, HEAD_DIM), lambda h: (0, h))
-    gain = pl.BlockSpec((1, HEAD_DIM), lambda h: (0, h))
+    gain = pl.BlockSpec((2, HEAD_DIM), lambda h: (0, h))
     pair = pl.BlockSpec((2, tokens, HEAD_DIM), lambda h: (0, 0, h))
     glob = pl.BlockSpec((2, count, HEAD_DIM), lambda h: (0, 0, h))
     pair_shape = (2, tokens, width)
@@ -407,7 +450,6 @@
             whole,
             whole,
             gain,
-            gain,
             flat,
             flat,
             flat,
@@ -424,76 +466,112 @@
             pltpu.VMEM((3 * tokens, HEAD_DIM), jnp.float32),
             pltpu.VMEM((3 * tokens, HEAD_DIM), jnp.float32),
             pltpu.VMEM((4 * tokens, HEAD_DIM), jnp.float32),
+            pltpu.VMEM((8, count), jnp.float32),
         ],
-    )(starts, live, totals, near, qgain, kgain, query, out_grad, key, val, window, globs)
+    )(tiles, readers, totals, near, gains, query, out_grad, key, val, window, globs)
+
+
+def finish_kernel(
+    ids_ref, tot_ref, sum_ref, dots_ref, near_ref, extra_ref, gain_ref,
+    q_ref, k_ref, dq_ref, own_ref, from_ref, qg_ref, kg_ref, vg_ref, lines,
+):
+    tokens = q_ref.shape[0]
+    device = lax.axis_index("ctx")
+    z = lax.rem(device // LOW, ZN)
+    spots = lax.broadcasted_iota(jnp.int32, (tokens, HEAD_DIM), 0) + device * tokens
+
+    @pl.when(pl.program_id(0) == 0)
+    def _():
+        inverse = lax.rsqrt(tot_ref[...] / D + EPSILON)
+        dots = dots_ref[...]
+        key_dots = dots[4:6] + near_ref[0, 6:8] + near_ref[1, 2:4]
+        rows = [inverse[0:1], inverse[1:2], inverse[2:3], inverse[3:4]]
+        rows += [dots[0:1], dots[1:2], key_dots[0:1], key_dots[1:2]]
+        for index, row in enumerate(rows):
+            lines[index * TILE : (index + 1) * TILE] = jnp.broadcast_to(row, (TILE, TILE)).T
+        for index in range(G_DEV):
+            extra = jnp.where(z == 0, extra_ref[index : index + 1], extra_ref[G_DEV + index : G_DEV + index + 1])
+            lines[3 * tokens :] += jnp.where(spots == ids_ref[index], extra, 0.0)
+
+    home_key = own_ref[0] + from_ref[0, 0].astype(jnp.float32) + from_ref[1, 0].astype(jnp.float32)
+    home_val = own_ref[1] + from_ref[0, 1].astype(jnp.float32) + from_ref[1, 1].astype(jnp.float32)
+    each = ZN * G_DEV
+    for index in range(G_DEV):
+        here = spots == ids_ref[index]
+        other = G_DEV + index
+        add_key = jnp.where(z == 0, sum_ref[index : index + 1], sum_ref[other : other + 1])
+        add_val = jnp.where(
+            z == 0, sum_ref[each + index : each + index + 1], sum_ref[each + other : each + other + 1]
+        )
+        home_key = home_key + jnp.where(here, add_key, 0.0)
+        home_val = home_val + jnp.where(here, add_val, 0.0)
+    query_inv = lines[0:tokens]
+    key_inv = lines[tokens : 2 * tokens]
+    query_dot = lines[2 * tokens : 3 * tokens]
+    key_dot = lines[3 * tokens :]
+    qg_ref[...] = (
+        query_inv * (gain_ref[0:1] * dq_ref[...])
+        - q_ref[...].astype(jnp.float32) * (query_inv * query_inv * query_inv) * (query_dot / D)
+    ).astype(jnp.bfloat16)
+    kg_ref[...] = (
+        key_inv * (gain_ref[1:2] * home_key)
+        - k_ref[...].astype(jnp.float32) * (key_inv * key_inv * key_inv) * (key_dot / D)
+    ).astype(jnp.bfloat16)
+    vg_ref[...] = home_val.astype(jnp.bfloat16)
+
+
+def finish(ids, totals, reduced, dots, near, extra, gains, query, key, dq, own, arrived):
+    tokens, width = query.shape
+    whole = pl.BlockSpec(memory_space=pltpu.VMEM)
+    flat = pl.BlockSpec((tokens, HEAD_DIM), lambda h: (0, h))
+
+    def rows(count):
+        return pl.BlockSpec((count, HEAD_DIM), lambda h: (0, h))
+
+    return pl.pallas_call(
+        finish_kernel,
+        grid=(width // HEAD_DIM,),
+        out_shape=(jax.ShapeDtypeStruct((tokens, width), jnp.bfloat16),) * 3,
+        in_specs=[
+            pl.BlockSpec(memory_space=pltpu.SMEM),
+            whole,
+            rows(reduced.shape[0]),
+            whole,
+            whole,
+            whole,
+            rows(2),
+            flat,
+            flat,
+            flat,
+            pl.BlockSpec((2, tokens, HEAD_DIM), lambda h: (0, 0, h)),
+            pl.BlockSpec((2, 2, tokens, HEAD_DIM), lambda h: (0, 0, 0, h)),
+        ],
+        out_specs=(flat,) * 3,
+        scratch_shapes=[pltpu.VMEM((4 * tokens, HEAD_DIM), jnp.float32)],
+    )(ids, totals, reduced, dots, near, extra, gains, query, key, dq, own, arrived)
 
 
 def body(
     query_raw, key_raw, values, out_grad, query_gain, key_gain, key_tiles, global_ids, readers
 ):
-    tokens_here, width = query_raw.shape
-    tiles_here = tokens_here // TILE
+    width = query_raw.shape[1]
     count = lax.axis_size("ctx")
-    yn = count // (LOW * ZN)
-    device = lax.axis_index("ctx")
-    query_rows = query_raw.astype(jnp.float32)
-    key_rows = key_raw.astype(jnp.float32)
-    own_rows = global_ids - device * tokens_here
-    own_keys = key_raw[own_rows].astype(jnp.float32)
-    own_vals = values[own_rows].astype(jnp.float32)
-    own_squares = jnp.sum(own_keys * own_keys, axis=1)
-    squares = jnp.concatenate(
-        [
-            jnp.sum(query_rows * query_rows, axis=1).reshape(tiles_here, TILE),
-            jnp.sum(key_rows * key_rows, axis=1).reshape(tiles_here, TILE),
-            jnp.broadcast_to(own_squares[:, None], (G_DEV, TILE)),
-            jnp.zeros((G_DEV, TILE), jnp.float32),
-        ]
+    gains = jnp.stack([query_gain, key_gain])
+    window, globs, totals, near = spread(global_ids, query_raw, key_raw, values, gains)
+    globs = (
+        globs.reshape(count, 2, G_DEV, width).transpose(1, 0, 2, 3).reshape(2, count * G_DEV, width)
     )
-    qgain = query_gain[None, :]
-    kgain = key_gain[None, :]
-    window, globs, totals, near = spread(
-        key_raw, values, squares, jnp.concatenate([own_keys, own_vals]), kgain
+    grad_query, to_prev, to_next, own_grads, glob_grads, dots = attention(
+        key_tiles, readers, totals, near, gains, query_raw, out_grad, key_raw, values, window, globs
     )
-    globs = (
-        globs.reshape(LOW, yn, ZN, 2, G_DEV, width)
-        .transpose(3, 1, 2, 0, 4, 5)
-        .reshape(2, count * G_DEV, width)
+    parts = glob_grads.reshape(2, LOW, -1, width)
+    arrived, reduced, dot_totals, dot_near, extra = collect(
+        global_ids, to_prev, to_next, parts, dots, key_raw, gains
     )
-    live = jnp.repeat(readers, G_DEV, axis=1)
-    starts = jnp.clip(key_tiles[:, 0] - (device - 1) * tiles_here, 0, 3 * tiles_here - KEYS)
-    grad_query, to_prev, to_next, own_grads, glob_grads, dots = attention(
-        starts, live, totals, near, qgain, kgain, query_raw, out_grad, key_raw, values, window, globs
-    )
-    parts = (
-        glob_grads.reshape(2, yn, ZN, LOW, G_DEV, width)
-        .transpose(3, 1, 2, 0, 4, 5)
-        .reshape(LOW, yn, ZN * 2 * G_DEV, width)
-    )
-    z = lax.rem(device // LOW, ZN)
-    weight = jnp.where(
-        (jnp.arange(ZN)[:, None] == z)[:, :, None, None] & (jnp.arange(2) == 0)[None, :, None, None],
-        (own_keys * key_gain)[None, None],
-        0.0,
-    ).reshape(ZN * 2 * G_DEV, width)
-    arrived, reduced, dot_totals, dot_near, extra = collect(to_prev, to_next, parts, dots, weight)
-    mine = lax.dynamic_index_in_dim(
-        reduced.reshape(ZN, 2, G_DEV, width), z, 0, keepdims=False
-    )
-    extra = extra.reshape(ZN, 2, G_DEV, 128)[:, 0, :, 0].sum(axis=0)
-    home = own_grads + arrived[0].astype(jnp.float32) + arrived[1].astype(jnp.float32)
-    spots = jnp.arange(tokens_here, dtype=jnp.int32)
-    query_dot = dot_totals[0:2].reshape(-1)
-    key_dot = (dot_totals[4:6] + dot_near[0, 6:8] + dot_near[1, 2:4]).reshape(-1)
-    for index in range(G_DEV):
-        here = spots == own_rows[index]
-        home = home + jnp.where(here[:, None], mine[:, index][:, None, :], 0.0)
-        key_dot = key_dot + jnp.where(here, extra[index], 0.0)
-    query_inv = lax.rsqrt(totals[0:2].reshape(-1, 1) / D + EPSILON)
-    key_inv = lax.rsqrt(totals[2:4].reshape(-1, 1) / D + EPSILON)
-    query_grad = norm_grad(query_rows, query_inv, grad_query * query_gain, query_dot)
-    key_grad = norm_grad(key_rows, key_inv, home[0] * key_gain, key_dot)
-    return (query_grad, key_grad, home[1].astype(jnp.bfloat16))
+    return tuple(finish(
+        global_ids, totals, reduced, dot_totals, dot_near, extra, gains,
+        query_raw, key_raw, grad_query, own_grads, arrived,
+    ))
 
 
 def solution(mesh):

time: 164 us -> 145 us (0.88)
  the two profiles are of different devices: /device:TPU:7 before, /device:TPU:32 now
where the time goes in v3:
time: 145 us; the launch traced here: 144 us
  Pallas kernels  140 us (97%)
  local copies, waits for them, and re-layouts  3.55 us (2%)
    pallas_call x1, Pallas kernels, spread(): pl.pallas_call(functools.partial(spread_kernel, count, heads), out_shape=...  61.2 us
    pallas_call x1, Pallas kernels, collect(): pl.pallas_call(functools.partial(collect_kernel, count, heads), out_shape...  60.9 us
    pallas_call x1, Pallas kernels, attention(): pl.pallas_call(attention_kernel, grid=(width // HEAD_DIM,), out_shape=(ja...  12.4 us
    pallas_call x1, Pallas kernels, finish(): pl.pallas_call(finish_kernel, grid=(width // HEAD_DIM,), out_shape=(jax.S...  5.16 us

profile of v3, /device:TPU:32, one launch (start us, length us, event | category | flops | bytes accessed | tf_op | source)
XLA Modules:
  0.0 144.4 jit_solution(3266629866322827356)
XLA Ops:
  0.6 0.7 stack.9
  1.3 0.7 stack.10
  2.0 0.6 pad_maximum_fusion.gain_ref
  2.6 61.2 %shard_map.112 = (bf16[2,2,256,640]{3,2,1,0:T(8,128)(2,1)}, bf16[8,4,2,4,640]{4,3,2,1,0:T(4,128)(2,1)}, f32[8,128]{1,0:T(8,128)}, f32[2,8,128]{2,1,0:T(8,128)}) custom-call(s32[2]{0:T(128)} %ids_ref.5, bf16[256,640]{1,0:T(8,128)(2,1)} %q_ref.3, bf16[256,640]{1,0:T(8,128)(2,1)} %k_ref.1, bf16[256,640]{1,0:T(8,128)(2,1)} %val_ref.3, ...), custom_call_target="tpu_custom_call" | custom-call | tf_op jit(solution)/shard_map/pallas_call | solution.py:186
  63.8 1.1 reshape.15
  64.9 0.2 copy.14
  65.1 0.8 reshape.16.glob_ref
  66.0 12.4 %shard_map.113 = (f32[256,640]{1,0:T(8,128)}, bf16[2,256,640]{2,1,0:T(8,128)(2,1)}, bf16[2,256,640]{2,1,0:T(8,128)(2,1)}, f32[2,256,640]{2,1,0:T(8,128)}, f32[2,128,640]{2,1,0:T(8,128)}, /*index=5*/f32[8,128]{1,0:T(8,128)}) custom-call(s32[2,4]{1,0:T(2,128)} %tiles_ref.1, s32[1,64]{1,0:T(1,128)} %readers_ref.1, f32[8,128]{1,0:T(8,128)} %get-tuple-element.18.tot_ref, ...), custom_call_target="tpu_custom_call" | custom-call | tf_op jit(solution)/shard_map/pallas_call | solution.py:436
  78.3 60.9 %shard_map.114 = (bf16[2,2,256,640]{3,2,1,0:T(8,128)(2,1)}, f32[8,640]{1,0:T(8,128)}, f32[8,128]{1,0:T(8,128)}, f32[2,8,128]{2,1,0:T(8,128)}, f32[8,128]{1,0:T(8,128)}) custom-call(s32[2]{0:T(128)} %ids_ref.5, bf16[2,256,640]{2,1,0:T(8,128)(2,1)} %get-tuple-element.22.prev_ref, bf16[2,256,640]{2,1,0:T(8,128)(2,1)} %get-tuple-element.23.next_ref, ...), custom_call_target="tpu_custom_call" | custom-call | tf_op jit(solution)/shard_map/pallas_call | solution.py:287
  139.3 5.2 %shard_map.115 = (bf16[256,640]{1,0:T(8,128)(2,1)}, bf16[256,640]{1,0:T(8,128)(2,1)}, bf16[256,640]{1,0:T(8,128)(2,1)}) custom-call(s32[2]{0:T(128)} %ids_ref.5, f32[8,128]{1,0:T(8,128)} %get-tuple-element.18.tot_ref, f32[8,640]{1,0:T(8,128)} %get-tuple-element.26.sum_ref, f32[8,128]{1,0:T(8,128)} %get-tuple-element.27.dots_ref, ...), custom_call_target="tpu_custom_call" | custom-call | tf_op jit(solution)/shard_map/pallas_call | solution.py:531

commit v4 on v3

--- a/solution.py
+++ b/solution.py
@@ -100,23 +100,27 @@
 
 
 def spread_kernel(
-    count, heads, ids_ref, query_ref, key_ref, val_ref, gain_ref,
-    win_ref, glob_ref, tot_ref, near_ref,
+    count, heads, ids_ref, query_ref, key_ref, val_ref, qgain_ref, kgain_ref,
+    win_ref, glob_ref, tot_ref, near_ref, gain_ref,
     sq_buf, hslots, total_buf, near_buf, own_buf, wsend, wrecv, hsend, hrecv, gsend, grecv, lsem,
 ):
     y, z, low, yn, other_z, y_peers, low_peers, after, before = places(count)
     peers = head_peers(heads)
     greet(peers + [after, before, other_z] + y_peers + low_peers)
     wsems, hsems, gsems = (wsend, wrecv), (hsend, hrecv), (gsend, grecv)
+    tokens, width = key_ref.shape
+    early = pl.ds(0, TILE)
+    rest = pl.ds(TILE, tokens - TILE)
     moved = [
-        remote(key_ref, win_ref.at[0, 0], wsems, 0, after),
-        remote(key_ref, win_ref.at[1, 0], wsems, 1, before),
-        remote(val_ref, win_ref.at[0, 1], wsems, 2, after),
-        remote(val_ref, win_ref.at[1, 1], wsems, 3, before),
+        remote(key_ref.at[early], win_ref.at[0, 0, early], wsems, 0, after),
+        remote(key_ref.at[early], win_ref.at[1, 0, early], wsems, 1, before),
+        remote(key_ref.at[rest], win_ref.at[0, 0, rest], wsems, 2, after),
+        remote(key_ref.at[rest], win_ref.at[1, 0, rest], wsems, 3, before),
+        remote(val_ref, win_ref.at[0, 1], wsems, 4, after),
+        remote(val_ref, win_ref.at[1, 1], wsems, 5, before),
     ]
-    for copy in moved:
-        copy.start()
-    tokens, width = key_ref.shape
+    for copy in moved[:2]:
+        copy.start()
     first = lax.axis_index("ctx") * tokens
     line = 0
     for ref in (query_ref, key_ref):
@@ -127,6 +131,9 @@
                 folded = folded + block * block
             sq_buf[line : line + 1] = jnp.sum(folded.T, axis=0, keepdims=True)
             line += 1
+    kgain = kgain_ref[...].reshape(1, width)
+    gain_ref[0:1] = qgain_ref[...].reshape(1, width)
+    gain_ref[1:2] = kgain
     raw = own_tokens(ids_ref, first, key_ref, val_ref)
     own_squares = jnp.sum(raw * raw, axis=1, keepdims=True)
     sq_buf[4:8] = jnp.broadcast_to(own_squares, (4, TILE))
@@ -137,16 +144,16 @@
     tot_ref[...] = total
     inverse = lax.rsqrt(total[4:8, 0:1] / D + EPSILON)
     is_key = lax.broadcasted_iota(jnp.int32, raw.shape, 0) < G_DEV
-    own_buf[...] = jnp.where(is_key, raw * inverse * gain_ref[1:2], raw).astype(jnp.bfloat16)
+    own_buf[...] = jnp.where(is_key, raw * inverse * kgain, raw).astype(jnp.bfloat16)
     swap = remote(own_buf, glob_ref.at[low, y, z], gsems, 0, other_z)
     swap.start()
     local = pltpu.make_async_copy(own_buf, glob_ref.at[low, y, z], lsem)
     local.start()
     near = [
-        remote(total_buf, near_buf.at[0], wsems, 4, after),
-        remote(total_buf, near_buf.at[1], wsems, 5, before),
+        remote(total_buf, near_buf.at[0], wsems, 6, after),
+        remote(total_buf, near_buf.at[1], wsems, 7, before),
     ]
-    for copy in near:
+    for copy in near + moved[2:]:
         copy.start()
     local.wait()
     remote(own_buf, glob_ref.at[low, y, 1 - z], gsems, 0, other_z).wait_recv()
@@ -174,7 +181,7 @@
         copy.wait_send()
 
 
-def spread(ids, query_raw, key_raw, values, gains):
+def spread(ids, query_raw, key_raw, values, query_gain, key_gain):
     count = lax.axis_size("ctx")
     heads = lax.axis_size("head")
     yn = count // (LOW * ZN)
@@ -190,17 +197,18 @@
             jax.ShapeDtypeStruct((LOW, yn, ZN, 2 * G_DEV, width), jnp.bfloat16),
             jax.ShapeDtypeStruct(lines, jnp.float32),
             jax.ShapeDtypeStruct((2,) + lines, jnp.float32),
+            jax.ShapeDtypeStruct((2, width), jnp.float32),
         ),
-        in_specs=[pl.BlockSpec(memory_space=pltpu.SMEM), vmem, vmem, vmem, vmem],
-        out_specs=(free, free, vmem, vmem),
+        in_specs=[pl.BlockSpec(memory_space=pltpu.SMEM), vmem, vmem, vmem, vmem, vmem],
+        out_specs=(free, free, vmem, vmem, vmem),
         scratch_shapes=[
             pltpu.VMEM(lines, jnp.float32),
             pltpu.VMEM((heads - 1,) + lines, jnp.float32),
             pltpu.VMEM(lines, jnp.float32),
             pltpu.VMEM((2,) + lines, jnp.float32),
             pltpu.VMEM((2 * G_DEV, width), jnp.bfloat16),
-            pltpu.SemaphoreType.DMA((6,)),
-            pltpu.SemaphoreType.DMA((6,)),
+            pltpu.SemaphoreType.DMA((8,)),
+            pltpu.SemaphoreType.DMA((8,)),
             pltpu.SemaphoreType.DMA((heads - 1,)),
             pltpu.SemaphoreType.DMA((heads - 1,)),
             pltpu.SemaphoreType.DMA((copies,)),
@@ -208,7 +216,7 @@
             pltpu.SemaphoreType.DMA,
         ],
         compiler_params=pltpu.CompilerParams(collective_id=1, has_side_effects=True),
-    )(ids, query_raw, key_raw, values, gains)
+    )(ids, query_raw, key_raw, values, query_gain, key_gain)
 
 
 def collect_kernel(
@@ -227,11 +235,18 @@
         copy = remote(part_ref.at[:, lax.rem(low + 1 + o, LOW)], slots.at[o], gsems, o, peer)
         copy.start()
         sent.append(copy)
+    tokens = key_ref.shape[0]
+    upper = pl.ds(0, TILE)
+    lower = pl.ds(TILE, tokens - TILE)
     moved = [
-        remote(next_ref, from_ref.at[0], wsems, 0, after),
-        remote(prev_ref, from_ref.at[1], wsems, 1, before),
+        remote(next_ref.at[0], from_ref.at[0, 0], wsems, 0, after),
+        remote(prev_ref.at[0], from_ref.at[1, 0], wsems, 1, before),
+        remote(next_ref.at[1, upper], from_ref.at[0, 1, upper], wsems, 4, after),
+        remote(prev_ref.at[1, upper], from_ref.at[1, 1, upper], wsems, 5, before),
+        remote(next_ref.at[1, lower], from_ref.at[0, 1, lower], wsems, 6, after),
+        remote(prev_ref.at[1, lower], from_ref.at[1, 1, lower], wsems, 7, before),
     ]
-    for copy in moved:
+    for copy in moved[:2]:
         copy.start()
     total = add_arrivals(dots_ref[...], hslots, dotted)
     total_buf[...] = total
@@ -242,7 +257,6 @@
     ]
     for copy in near:
         copy.start()
-    tokens = key_ref.shape[0]
     raw = own_tokens(ids_ref, lax.axis_index("ctx") * tokens, key_ref, key_ref) * gain_ref[1:2]
     summed = add_arrivals(part_ref[:, low], slots, sent)
     each = ZN * G_DEV
@@ -257,7 +271,8 @@
     row = add_arrivals(half[y], yslots, ysent)
     quarter[...] = row
     swap = remote(quarter, zslot, gsems, LOW - 1 + yn - 1, other_z)
-    swap.start()
+    for copy in [swap] + moved[2:4]:
+        copy.start()
     swap.wait_recv()
     reduced = row + zslot[...]
     sum_ref[...] = reduced
@@ -265,6 +280,8 @@
     extra = jnp.broadcast_to(jnp.concatenate([share, share]), extra_buf.shape)
     extra_buf[...] = extra
     extras = start_all(extra_buf, eslots, esems, peers)
+    for copy in moved[4:]:
+        copy.start()
     extra_ref[...] = add_arrivals(extra, eslots, extras)
     for copy in near:
         copy.wait()
@@ -306,8 +323,8 @@
             pltpu.VMEM((2,) + dots.shape, jnp.float32),
             pltpu.VMEM((rows, 128), jnp.float32),
             pltpu.VMEM((heads - 1, rows, 128), jnp.float32),
-            pltpu.SemaphoreType.DMA((4,)),
-            pltpu.SemaphoreType.DMA((4,)),
+            pltpu.SemaphoreType.DMA((8,)),
+            pltpu.SemaphoreType.DMA((8,)),
             pltpu.SemaphoreType.DMA((copies,)),
             pltpu.SemaphoreType.DMA((copies,)),
             pltpu.SemaphoreType.DMA((heads - 1,)),
@@ -556,8 +573,9 @@
 ):
     width = query_raw.shape[1]
     count = lax.axis_size("ctx")
-    gains = jnp.stack([query_gain, key_gain])
-    window, globs, totals, near = spread(global_ids, query_raw, key_raw, values, gains)
+    window, globs, totals, near, gains = spread(
+        global_ids, query_raw, key_raw, values, query_gain, key_gain
+    )
     globs = (
         globs.reshape(count, 2, G_DEV, width).transpose(1, 0, 2, 3).reshape(2, count * G_DEV, width)
     )

time: 145 us -> 134 us (0.924)
  the two profiles are of different devices: /device:TPU:32 before, /device:TPU:103 now
where the time goes in v4:
time: 134 us
  Pallas kernels  131 us (98%)
  local copies, waits for them, and re-layouts  2.17 us (2%)
    pallas_call x1, Pallas kernels, collect(): pl.pallas_call(functools.partial(collect_kernel, count, heads), out_shape...  66.7 us
    pallas_call x1, Pallas kernels, spread(): pl.pallas_call(functools.partial(spread_kernel, count, heads), out_shape=...  46.9 us
    pallas_call x1, Pallas kernels, attention(): pl.pallas_call(attention_kernel, grid=(width // HEAD_DIM,), out_shape=(ja...  12.4 us
    pallas_call x1, Pallas kernels, finish(): pl.pallas_call(finish_kernel, grid=(width // HEAD_DIM,), out_shape=(jax.S...  5.16 us

profile of v4, /device:TPU:103, one launch (start us, length us, event | category | flops | bytes accessed | tf_op | source)
XLA Modules:
  0.0 134.0 jit_solution(11137878161142327703)
XLA Ops:
  0.6 46.9 %shard_map.112 = (bf16[2,2,256,640]{3,2,1,0:T(8,128)(2,1)}, bf16[8,4,2,4,640]{4,3,2,1,0:T(4,128)(2,1)}, f32[8,128]{1,0:T(8,128)}, f32[2,8,128]{2,1,0:T(8,128)}, f32[2,640]{1,0:T(2,128)}) custom-call(s32[2]{0:T(128)} %ids_ref.5, bf16[256,640]{1,0:T(8,128)(2,1)} %q_ref.3, bf16[256,640]{1,0:T(8,128)(2,1)} %k_ref.1, bf16[256,640]{1,0:T(8,128)(2,1)} %val_ref.3, ...), custom_call_target="tpu_custom_call" | custom-call | tf_op jit(solution)/shard_map/pallas_call | solution.py:193
  47.6 1.1 reshape.15
  48.7 0.2 copy.14
  48.9 0.8 reshape.16.glob_ref
  49.8 12.4 %shard_map.113 = (f32[256,640]{1,0:T(8,128)}, bf16[2,256,640]{2,1,0:T(8,128)(2,1)}, bf16[2,256,640]{2,1,0:T(8,128)(2,1)}, f32[2,256,640]{2,1,0:T(8,128)}, f32[2,128,640]{2,1,0:T(8,128)}, /*index=5*/f32[8,128]{1,0:T(8,128)}) custom-call(s32[2,4]{1,0:T(2,128)} %tiles_ref.1, s32[1,64]{1,0:T(1,128)} %readers_ref.1, f32[8,128]{1,0:T(8,128)} %get-tuple-element.19.tot_ref, ...), custom_call_target="tpu_custom_call" | custom-call | tf_op jit(solution)/shard_map/pallas_call | solution.py:453
  62.1 66.7 %shard_map.114 = (bf16[2,2,256,640]{3,2,1,0:T(8,128)(2,1)}, f32[8,640]{1,0:T(8,128)}, f32[8,128]{1,0:T(8,128)}, f32[2,8,128]{2,1,0:T(8,128)}, f32[8,128]{1,0:T(8,128)}) custom-call(s32[2]{0:T(128)} %ids_ref.5, bf16[2,256,640]{2,1,0:T(8,128)(2,1)} %get-tuple-element.24.prev_ref, bf16[2,256,640]{2,1,0:T(8,128)(2,1)} %get-tuple-element.25.next_ref, ...), custom_call_target="tpu_custom_call" | custom-call | tf_op jit(solution)/shard_map/pallas_call | solution.py:304
  128.8 5.2 %shard_map.115 = (bf16[256,640]{1,0:T(8,128)(2,1)}, bf16[256,640]{1,0:T(8,128)(2,1)}, bf16[256,640]{1,0:T(8,128)(2,1)}) custom-call(s32[2]{0:T(128)} %ids_ref.5, f32[8,128]{1,0:T(8,128)} %get-tuple-element.19.tot_ref, f32[8,640]{1,0:T(8,128)} %get-tuple-element.28.sum_ref, f32[8,128]{1,0:T(8,128)} %get-tuple-element.29.dots_ref, ...), custom_call_target="tpu_custom_call" | custom-call | tf_op jit(solution)/shard_map/pallas_call | solution.py:548

commit v5 on v4

--- a/solution.py
+++ b/solution.py
@@ -109,8 +109,8 @@
     greet(peers + [after, before, other_z] + y_peers + low_peers)
     wsems, hsems, gsems = (wsend, wrecv), (hsend, hrecv), (gsend, grecv)
     tokens, width = key_ref.shape
-    early = pl.ds(0, TILE)
-    rest = pl.ds(TILE, tokens - TILE)
+    early = pl.ds(0, TILE // 2)
+    rest = pl.ds(TILE // 2, tokens - TILE // 2)
     moved = [
         remote(key_ref.at[early], win_ref.at[0, 0, early], wsems, 0, after),
         remote(key_ref.at[early], win_ref.at[1, 0, early], wsems, 1, before),
@@ -236,17 +236,11 @@
         copy.start()
         sent.append(copy)
     tokens = key_ref.shape[0]
-    upper = pl.ds(0, TILE)
-    lower = pl.ds(TILE, tokens - TILE)
     moved = [
-        remote(next_ref.at[0], from_ref.at[0, 0], wsems, 0, after),
-        remote(prev_ref.at[0], from_ref.at[1, 0], wsems, 1, before),
-        remote(next_ref.at[1, upper], from_ref.at[0, 1, upper], wsems, 4, after),
-        remote(prev_ref.at[1, upper], from_ref.at[1, 1, upper], wsems, 5, before),
-        remote(next_ref.at[1, lower], from_ref.at[0, 1, lower], wsems, 6, after),
-        remote(prev_ref.at[1, lower], from_ref.at[1, 1, lower], wsems, 7, before),
+        remote(next_ref, from_ref.at[0], wsems, 0, after),
+        remote(prev_ref, from_ref.at[1], wsems, 1, before),
     ]
-    for copy in moved[:2]:
+    for copy in moved:
         copy.start()
     total = add_arrivals(dots_ref[...], hslots, dotted)
     total_buf[...] = total
@@ -271,8 +265,7 @@
     row = add_arrivals(half[y], yslots, ysent)
     quarter[...] = row
     swap = remote(quarter, zslot, gsems, LOW - 1 + yn - 1, other_z)
-    for copy in [swap] + moved[2:4]:
-        copy.start()
+    swap.start()
     swap.wait_recv()
     reduced = row + zslot[...]
     sum_ref[...] = reduced
@@ -280,8 +273,6 @@
     extra = jnp.broadcast_to(jnp.concatenate([share, share]), extra_buf.shape)
     extra_buf[...] = extra
     extras = start_all(extra_buf, eslots, esems, peers)
-    for copy in moved[4:]:
-        copy.start()
     extra_ref[...] = add_arrivals(extra, eslots, extras)
     for copy in near:
         copy.wait()

time: 134 us -> 136 us (1.015)
  the two profiles are of different devices: /device:TPU:103 before, /device:TPU:6 now
where the time goes in v5:
time: 136 us; the launch traced here: 135 us
  Pallas kernels  132 us (97%)
  local copies, waits for them, and re-layouts  2.17 us (2%)
    pallas_call x1, Pallas kernels, collect(): pl.pallas_call(functools.partial(collect_kernel, count, heads), out_shape...  74.2 us
    pallas_call x1, Pallas kernels, spread(): pl.pallas_call(functools.partial(spread_kernel, count, heads), out_shape=...  40.7 us
    pallas_call x1, Pallas kernels, attention(): pl.pallas_call(attention_kernel, grid=(width // HEAD_DIM,), out_shape=(ja...  12.4 us
    pallas_call x1, Pallas kernels, finish(): pl.pallas_call(finish_kernel, grid=(width // HEAD_DIM,), out_shape=(jax.S...  5.16 us

profile of v5, /device:TPU:6, one launch (start us, length us, event | category | flops | bytes accessed | tf_op | source)
XLA Modules:
  0.0 135.3 jit_solution(10130594255133746492)
XLA Ops:
  0.6 40.7 %shard_map.112 = (bf16[2,2,256,640]{3,2,1,0:T(8,128)(2,1)}, bf16[8,4,2,4,640]{4,3,2,1,0:T(4,128)(2,1)}, f32[8,128]{1,0:T(8,128)}, f32[2,8,128]{2,1,0:T(8,128)}, f32[2,640]{1,0:T(2,128)}) custom-call(s32[2]{0:T(128)} %ids_ref.5, bf16[256,640]{1,0:T(8,128)(2,1)} %q_ref.3, bf16[256,640]{1,0:T(8,128)(2,1)} %k_ref.1, bf16[256,640]{1,0:T(8,128)(2,1)} %val_ref.3, ...), custom_call_target="tpu_custom_call" | custom-call | tf_op jit(solution)/shard_map/pallas_call | solution.py:193
  41.3 1.1 reshape.15
  42.4 0.2 copy.14
  42.7 0.8 reshape.16.glob_ref
  43.5 12.4 %shard_map.113 = (f32[256,640]{1,0:T(8,128)}, bf16[2,256,640]{2,1,0:T(8,128)(2,1)}, bf16[2,256,640]{2,1,0:T(8,128)(2,1)}, f32[2,256,640]{2,1,0:T(8,128)}, f32[2,128,640]{2,1,0:T(8,128)}, /*index=5*/f32[8,128]{1,0:T(8,128)}) custom-call(s32[2,4]{1,0:T(2,128)} %tiles_ref.1, s32[1,64]{1,0:T(1,128)} %readers_ref.1, f32[8,128]{1,0:T(8,128)} %get-tuple-element.19.tot_ref, ...), custom_call_target="tpu_custom_call" | custom-call | tf_op jit(solution)/shard_map/pallas_call | solution.py:444
  55.9 74.2 %shard_map.114 = (bf16[2,2,256,640]{3,2,1,0:T(8,128)(2,1)}, f32[8,640]{1,0:T(8,128)}, f32[8,128]{1,0:T(8,128)}, f32[2,8,128]{2,1,0:T(8,128)}, f32[8,128]{1,0:T(8,128)}) custom-call(s32[2]{0:T(128)} %ids_ref.5, bf16[2,256,640]{2,1,0:T(8,128)(2,1)} %get-tuple-element.24.prev_ref, bf16[2,256,640]{2,1,0:T(8,128)(2,1)} %get-tuple-element.25.next_ref, ...), custom_call_target="tpu_custom_call" | custom-call | tf_op jit(solution)/shard_map/pallas_call | solution.py:295
  130.1 5.2 %shard_map.115 = (bf16[256,640]{1,0:T(8,128)(2,1)}, bf16[256,640]{1,0:T(8,128)(2,1)}, bf16[256,640]{1,0:T(8,128)(2,1)}) custom-call(s32[2]{0:T(128)} %ids_ref.5, f32[8,128]{1,0:T(8,128)} %get-tuple-element.19.tot_ref, f32[8,640]{1,0:T(8,128)} %get-tuple-element.28.sum_ref, f32[8,128]{1,0:T(8,128)} %get-tuple-element.29.dots_ref, ...), custom_call_target="tpu_custom_call" | custom-call | tf_op jit(solution)/shard_map/pallas_call | solution.py:539

commit v6 on v4

--- a/solution.py
+++ b/solution.py
@@ -62,7 +62,7 @@
 def add_arrivals(total, slots, copies):
     for o, copy in enumerate(copies):
         copy.wait_recv()
-        total = total + slots[o]
+        total = total + slots[o].astype(jnp.float32)
     return total
 
 
@@ -109,8 +109,8 @@
     greet(peers + [after, before, other_z] + y_peers + low_peers)
     wsems, hsems, gsems = (wsend, wrecv), (hsend, hrecv), (gsend, grecv)
     tokens, width = key_ref.shape
-    early = pl.ds(0, TILE)
-    rest = pl.ds(TILE, tokens - TILE)
+    early = pl.ds(0, TILE // 2)
+    rest = pl.ds(TILE // 2, tokens - TILE // 2)
     moved = [
         remote(key_ref.at[early], win_ref.at[0, 0, early], wsems, 0, after),
         remote(key_ref.at[early], win_ref.at[1, 0, early], wsems, 1, before),
@@ -258,7 +258,7 @@
     for copy in near:
         copy.start()
     raw = own_tokens(ids_ref, lax.axis_index("ctx") * tokens, key_ref, key_ref) * gain_ref[1:2]
-    summed = add_arrivals(part_ref[:, low], slots, sent)
+    summed = add_arrivals(part_ref[:, low].astype(jnp.float32), slots, sent)
     each = ZN * G_DEV
     for row in range(yn):
         half[row, 0:each] = summed[0, row * each : (row + 1) * each]
@@ -313,7 +313,7 @@
         in_specs=[pl.BlockSpec(memory_space=pltpu.SMEM), free, free, vmem, vmem, vmem, vmem],
         out_specs=(free, vmem, vmem, vmem, vmem),
         scratch_shapes=[
-            pltpu.VMEM((LOW - 1, 2) + parts.shape[2:], jnp.float32),
+            pltpu.VMEM((LOW - 1, 2) + parts.shape[2:], jnp.bfloat16),
             pltpu.VMEM((yn, rows, width), jnp.float32),
             pltpu.VMEM((yn - 1, rows, width), jnp.float32),
             pltpu.VMEM((rows, width), jnp.float32),
@@ -424,8 +424,8 @@
         prev_ref[pair_index] = cat[0:tokens].astype(jnp.bfloat16)
         own_ref[pair_index] = cat[tokens : 2 * tokens]
         next_ref[pair_index] = cat[2 * tokens :].astype(jnp.bfloat16)
-    dglob_ref[0] = gdk
-    dglob_ref[1] = gdv
+    dglob_ref[0] = gdk.astype(jnp.bfloat16)
+    dglob_ref[1] = gdv.astype(jnp.bfloat16)
     dot_sums[0:tokens] += dq_ref[...] * qgain * query_rows
     for index, block in enumerate(blocks):
         rows = slice(index * tokens, (index + 1) * tokens)
@@ -458,7 +458,7 @@
             jax.ShapeDtypeStruct(pair_shape, jnp.bfloat16),
             jax.ShapeDtypeStruct(pair_shape, jnp.bfloat16),
             jax.ShapeDtypeStruct(pair_shape, jnp.float32),
-            jax.ShapeDtypeStruct((2, count, width), jnp.float32),
+            jax.ShapeDtypeStruct((2, count, width), jnp.bfloat16),
             jax.ShapeDtypeStruct((lines, TILE), jnp.float32),
         ),
         in_specs=[

time: 134 us -> 132 us (0.985)
  the two profiles are of different devices: /device:TPU:103 before, /device:TPU:96 now
where the time goes in v6:
time: 132 us
  Pallas kernels  129 us (98%)
  local copies, waits for them, and re-layouts  2.17 us (2%)
    pallas_call x1, Pallas kernels, collect(): pl.pallas_call(functools.partial(collect_kernel, count, heads), out_shape...  60.5 us
    pallas_call x1, Pallas kernels, spread(): pl.pallas_call(functools.partial(spread_kernel, count, heads), out_shape=...  50.7 us
    pallas_call x1, Pallas kernels, attention(): pl.pallas_call(attention_kernel, grid=(width // HEAD_DIM,), out_shape=(ja...  12.4 us
    pallas_call x1, Pallas kernels, finish(): pl.pallas_call(finish_kernel, grid=(width // HEAD_DIM,), out_shape=(jax.S...  5.16 us

profile of v6, /device:TPU:96, one launch (start us, length us, event | category | flops | bytes accessed | tf_op | source)
XLA Modules:
  0.0 131.5 jit_solution(1967419485056766809)
XLA Ops:
  0.6 50.7 %shard_map.112 = (bf16[2,2,256,640]{3,2,1,0:T(8,128)(2,1)}, bf16[8,4,2,4,640]{4,3,2,1,0:T(4,128)(2,1)}, f32[8,128]{1,0:T(8,128)}, f32[2,8,128]{2,1,0:T(8,128)}, f32[2,640]{1,0:T(2,128)}) custom-call(s32[2]{0:T(128)} %ids_ref.5, bf16[256,640]{1,0:T(8,128)(2,1)} %q_ref.3, bf16[256,640]{1,0:T(8,128)(2,1)} %k_ref.1, bf16[256,640]{1,0:T(8,128)(2,1)} %val_ref.3, ...), custom_call_target="tpu_custom_call" | custom-call | tf_op jit(solution)/shard_map/pallas_call | solution.py:193
  51.3 1.1 reshape.15
  52.4 0.2 copy.14
  52.6 0.8 reshape.16.glob_ref
  53.5 12.4 %shard_map.113 = (f32[256,640]{1,0:T(8,128)}, bf16[2,256,640]{2,1,0:T(8,128)(2,1)}, bf16[2,256,640]{2,1,0:T(8,128)(2,1)}, f32[2,256,640]{2,1,0:T(8,128)}, bf16[2...) custom-call(s32[2,4]{1,0:T(2,128)} %tiles_ref.1, s32[1,64]{1,0:T(1,128)} %readers_ref.1, f32[8,128]{1,0:T(8,128)} %get-tuple-element.19.tot_ref, ...), custom_call_target="tpu_custom_call" | custom-call | tf_op jit(solution)/shard_map/pallas_call | solution.py:453
  65.9 60.5 %shard_map.114 = (bf16[2,2,256,640]{3,2,1,0:T(8,128)(2,1)}, f32[8,640]{1,0:T(8,128)}, f32[8,128]{1,0:T(8,128)}, f32[2,8,128]{2,1,0:T(8,128)}, f32[8,128]{1,0:T(8,128)}) custom-call(s32[2]{0:T(128)} %ids_ref.5, bf16[2,256,640]{2,1,0:T(8,128)(2,1)} %get-tuple-element.24.prev_ref, bf16[2,256,640]{2,1,0:T(8,128)(2,1)} %get-tuple-element.25.next_ref, ...), custom_call_target="tpu_custom_call" | custom-call | tf_op jit(solution)/shard_map/pallas_call | solution.py:304
  126.4 5.2 %shard_map.115 = (bf16[256,640]{1,0:T(8,128)(2,1)}, bf16[256,640]{1,0:T(8,128)(2,1)}, bf16[256,640]{1,0:T(8,128)(2,1)}) custom-call(s32[2]{0:T(128)} %ids_ref.5, f32[8,128]{1,0:T(8,128)} %get-tuple-element.19.tot_ref, f32[8,640]{1,0:T(8,128)} %get-tuple-element.28.sum_ref, f32[8,128]{1,0:T(8,128)} %get-tuple-element.29.dots_ref, ...), custom_call_target="tpu_custom_call" | custom-call | tf_op jit(solution)/shard_map/pallas_call | solution.py:548

commit v7 on v6

--- a/solution.py
+++ b/solution.py
@@ -271,7 +271,7 @@
     row = add_arrivals(half[y], yslots, ysent)
     quarter[...] = row
     swap = remote(quarter, zslot, gsems, LOW - 1 + yn - 1, other_z)
-    for copy in [swap] + moved[2:4]:
+    for copy in [swap] + moved[2:]:
         copy.start()
     swap.wait_recv()
     reduced = row + zslot[...]
@@ -280,8 +280,6 @@
     extra = jnp.broadcast_to(jnp.concatenate([share, share]), extra_buf.shape)
     extra_buf[...] = extra
     extras = start_all(extra_buf, eslots, esems, peers)
-    for copy in moved[4:]:
-        copy.start()
     extra_ref[...] = add_arrivals(extra, eslots, extras)
     for copy in near:
         copy.wait()

time: 132 us -> 133 us (level)
  the two profiles are of different devices: /device:TPU:96 before, /device:TPU:104 now
where the time goes in v7:
time: 133 us
  Pallas kernels  130 us (98%)
  local copies, waits for them, and re-layouts  2.17 us (2%)
    pallas_call x1, Pallas kernels, collect(): pl.pallas_call(functools.partial(collect_kernel, count, heads), out_shape...  65.4 us
    pallas_call x1, Pallas kernels, spread(): pl.pallas_call(functools.partial(spread_kernel, count, heads), out_shape=...  46.8 us
    pallas_call x1, Pallas kernels, attention(): pl.pallas_call(attention_kernel, grid=(width // HEAD_DIM,), out_shape=(ja...  12.3 us
    pallas_call x1, Pallas kernels, finish(): pl.pallas_call(finish_kernel, grid=(width // HEAD_DIM,), out_shape=(jax.S...  5.16 us

profile of v7, /device:TPU:104, one launch (start us, length us, event | category | flops | bytes accessed | tf_op | source)
XLA Modules:
  0.0 132.5 jit_solution(9640595561369761054)
XLA Ops:
  0.6 46.8 %shard_map.112 = (bf16[2,2,256,640]{3,2,1,0:T(8,128)(2,1)}, bf16[8,4,2,4,640]{4,3,2,1,0:T(4,128)(2,1)}, f32[8,128]{1,0:T(8,128)}, f32[2,8,128]{2,1,0:T(8,128)}, f32[2,640]{1,0:T(2,128)}) custom-call(s32[2]{0:T(128)} %ids_ref.5, bf16[256,640]{1,0:T(8,128)(2,1)} %q_ref.3, bf16[256,640]{1,0:T(8,128)(2,1)} %k_ref.1, bf16[256,640]{1,0:T(8,128)(2,1)} %val_ref.3, ...), custom_call_target="tpu_custom_call" | custom-call | tf_op jit(solution)/shard_map/pallas_call | solution.py:193
  47.5 1.1 reshape.15
  48.6 0.2 copy.14
  48.8 0.8 reshape.16.glob_ref
  49.7 12.3 %shard_map.113 = (f32[256,640]{1,0:T(8,128)}, bf16[2,256,640]{2,1,0:T(8,128)(2,1)}, bf16[2,256,640]{2,1,0:T(8,128)(2,1)}, f32[2,256,640]{2,1,0:T(8,128)}, bf16[2...) custom-call(s32[2,4]{1,0:T(2,128)} %tiles_ref.1, s32[1,64]{1,0:T(1,128)} %readers_ref.1, f32[8,128]{1,0:T(8,128)} %get-tuple-element.19.tot_ref, ...), custom_call_target="tpu_custom_call" | custom-call | tf_op jit(solution)/shard_map/pallas_call | solution.py:451
  62.0 65.4 %shard_map.114 = (bf16[2,2,256,640]{3,2,1,0:T(8,128)(2,1)}, f32[8,640]{1,0:T(8,128)}, f32[8,128]{1,0:T(8,128)}, f32[2,8,128]{2,1,0:T(8,128)}, f32[8,128]{1,0:T(8,128)}) custom-call(s32[2]{0:T(128)} %ids_ref.5, bf16[2,256,640]{2,1,0:T(8,128)(2,1)} %get-tuple-element.24.prev_ref, bf16[2,256,640]{2,1,0:T(8,128)(2,1)} %get-tuple-element.25.next_ref, ...), custom_call_target="tpu_custom_call" | custom-call | tf_op jit(solution)/shard_map/pallas_call | solution.py:302
  127.4 5.2 %shard_map.115 = (bf16[256,640]{1,0:T(8,128)(2,1)}, bf16[256,640]{1,0:T(8,128)(2,1)}, bf16[256,640]{1,0:T(8,128)(2,1)}) custom-call(s32[2]{0:T(128)} %ids_ref.5, f32[8,128]{1,0:T(8,128)} %get-tuple-element.19.tot_ref, f32[8,640]{1,0:T(8,128)} %get-tuple-element.28.sum_ref, f32[8,128]{1,0:T(8,128)} %get-tuple-element.29.dots_ref, ...), custom_call_target="tpu_custom_call" | custom-call | tf_op jit(solution)/shard_map/pallas_call | solution.py:546
